TPU v7x, 256 devices: a whole 4x4x8 slice. The times are simulated.
256 devices in a mesh: freq: 16 (over x, y), space: 16 (over z, core).
Axes of the slice: x: 4, y: 4, z: 8, core: 2. Of those that a mesh axis runs over, the one named last changes fastest.
Arguments:
- spectra: bfloat16 [2, 256, 24, 65536], P(None, 'freq', None, 'space'), may hold values from -6 to 6
- eigvecs: bfloat16 [2, 256, 4, 65536], P(None, 'freq', None, 'space'), may hold values from -6 to 6
- weights: bfloat16 [65536], P('space'), may hold values from 0.19921875 to 5
Outputs:
- filtered: float32 [3200, 65536], P(None, ('space', 'freq'))
All inputs are finite; a program needn't handle non-finite values.
Results may differ from a plain program's by a relative error of at most 0.004.
Values may be sent and summed in bfloat16 or wider, within the bound.
No kernel may reach another device: no remote copies, remote signals or barrier semaphores. Data moves between devices by JAX's collectives and lax.ppermute only.
A program may use at most 64 MiB of HBM per device.

v0:
```python
import math

import jax
import jax.numpy as jnp
import numpy as np
from jax import lax
from jax.experimental import pallas as pl
from jax.experimental.pallas import tpu as pltpu
from jax.sharding import PartitionSpec as P

VMEM_LIMIT = 48 * 1024 * 1024


def cut_points(eigvecs, parts):
    width = eigvecs.shape[3] // parts

    def kernel(source, pieces, done):
        copies = []
        for part in range(parts):
            columns = source.at[:, :, :, pl.ds(part * width, width)]
            copies.append(pltpu.make_async_copy(columns, pieces.at[part], done.at[part]))
        for copy in copies:
            copy.start()
        for copy in copies:
            copy.wait()

    return pl.pallas_call(
        kernel,
        out_shape=jax.ShapeDtypeStruct((parts, *eigvecs.shape[:3], width), eigvecs.dtype),
        in_specs=[pl.BlockSpec(memory_space=pl.ANY)],
        out_specs=pl.BlockSpec(memory_space=pl.ANY),
        scratch_shapes=[pltpu.SemaphoreType.DMA((parts,))],
        cost_estimate=pl.CostEstimate(
            flops=0, transcendentals=0, bytes_accessed=2 * eigvecs.size * eigvecs.dtype.itemsize
        ),
        name="cut_points",
    )(eigvecs)


def project(spectra, eigvecs, weights, per_step):
    _, freqs, blocks, points = spectra.shape
    modes = eigvecs.shape[2]
    half = freqs * modes
    steps = freqs // per_step

    def kernel(spectra_ref, eigvecs_ref, weights_ref, out_ref, terms):
        step = pl.program_id(0)

        @pl.when(step == 0)
        def _():
            terms[...] = jnp.zeros_like(terms)

        scale = weights_ref[...].astype(jnp.float32)
        rows = per_step * modes
        pieces = [[[], []], [[], []]]
        for k in range(per_step):
            weighted = jnp.concatenate(
                [
                    (eigvecs_ref[part, k].astype(jnp.float32) * scale).astype(jnp.bfloat16)
                    for part in range(2)
                ],
                axis=0,
            )
            for part in range(2):
                product = lax.dot_general(
                    weighted,
                    spectra_ref[part, k],
                    (((1,), (1,)), ((), ())),
                    preferred_element_type=jnp.float32,
                )
                for kind in range(2):
                    pieces[part][kind].append(product[kind * modes : (kind + 1) * modes])
        for part in range(2):
            for kind in range(2):
                first = pl.multiple_of(kind * half + step * rows, 8)
                terms[part, pl.ds(first, rows), :blocks] = jnp.concatenate(
                    pieces[part][kind], axis=0
                )

        @pl.when(step == steps - 1)
        def _():
            of_real = jnp.transpose(terms[0])[:blocks]
            of_imag = pltpu.roll(jnp.transpose(terms[1])[:blocks], half, 1)
            lane = lax.broadcasted_iota(jnp.int32, of_real.shape, 1)
            out_ref[...] = jnp.where(lane < half, of_real, -of_real) + of_imag

    return pl.pallas_call(
        kernel,
        grid=(steps,),
        out_shape=jax.ShapeDtypeStruct((blocks, 2 * half), jnp.float32),
        in_specs=[
            pl.BlockSpec((2, per_step, blocks, points), lambda i: (0, i, 0, 0)),
            pl.BlockSpec((2, per_step, modes, points), lambda i: (0, i, 0, 0)),
            pl.BlockSpec((1, points), lambda i: (0, 0)),
        ],
        out_specs=pl.BlockSpec((blocks, 2 * half), lambda i: (0, 0)),
        scratch_shapes=[pltpu.VMEM((2, 2 * half, 2 * half), jnp.float32)],
        compiler_params=pltpu.CompilerParams(vmem_limit_bytes=VMEM_LIMIT),
        cost_estimate=pl.CostEstimate(
            flops=8 * freqs * blocks * modes * points,
            transcendentals=0,
            bytes_accessed=2 * (spectra.size + eigvecs.size),
        ),
        name="project",
    )(spectra, eigvecs, weights.reshape(1, points))


def transform_table(length, groups):
    sample = np.arange(length)
    phase = 2.0 * np.pi * ((sample[:, None] * sample[None, :]) % length) / length
    window = np.sin(np.pi * (sample + 0.5) / length) / math.sqrt(length)
    table = np.stack([np.cos(phase), -np.sin(phase)], axis=1) * window[:, None, None]
    table = table.reshape(length, 2, groups, length // groups).transpose(0, 2, 1, 3)
    return jnp.asarray(table.reshape(length, 2 * length), jnp.bfloat16)


def synthesize(coefficients, moved_modes, table):
    groups, blocks, lanes = coefficients.shape
    columns = moved_modes.shape[2]
    length = table.shape[0]
    freqs = length // groups
    modes = lanes // (2 * freqs)
    half_lanes = lanes // 2
    half = length // 2

    def kernel(coef_ref, modes_ref, table_ref, out_ref, high, low, rebuilt, result, done):
        lane = lax.broadcasted_iota(jnp.int32, (freqs, lanes), 1)
        row = lax.broadcasted_iota(jnp.int32, (freqs, lanes), 0)
        own = jnp.where((lane % half_lanes) // modes == row, 1.0, 0.0)
        signed = jnp.where(lane < half_lanes, own, -own)
        for group in range(groups):
            plain = coef_ref[group]
            for kind, value in enumerate((plain, pltpu.roll(plain, half_lanes, 1))):
                rounded = value.astype(jnp.bfloat16).astype(jnp.float32)
                high[kind, group] = rounded
                low[kind, group] = value - rounded
        for group in range(groups):
            tiles = []
            for block in range(blocks):
                for kind, mask in enumerate((signed, own)):
                    tiles.append(
                        jnp.concatenate(
                            [
                                (jnp.broadcast_to(
                                    side[kind, group, pl.ds(block, 1), :], (freqs, lanes)
                                ) * mask).astype(jnp.bfloat16)
                                for side in (high, low)
                            ],
                            axis=1,
                        )
                    )
            values = modes_ref[group]
            product = jnp.dot(
                jnp.concatenate(tiles, axis=0),
                jnp.concatenate([values, values], axis=0),
                preferred_element_type=jnp.float32,
            )
            rebuilt[:, group * 2 * freqs : (group + 1) * 2 * freqs, :] = product.astype(
                jnp.bfloat16
            ).reshape(blocks, 2 * freqs, columns)
        result[0] = jnp.zeros((half, columns), jnp.float32)

        def send(block):
            return pltpu.make_async_copy(result.at[block], out_ref.at[block], done.at[block])

        for block in range(blocks):
            series = jnp.dot(table_ref[...], rebuilt[block], preferred_element_type=jnp.float32)
            result[block] += series[:half]
            result[block + 1] = series[half:]
            send(block).start()
        send(blocks).start()
        for block in range(blocks + 1):
            send(block).wait()

    return pl.pallas_call(
        kernel,
        out_shape=jax.ShapeDtypeStruct((blocks + 1, half, columns), jnp.float32),
        in_specs=[pl.BlockSpec(memory_space=pltpu.VMEM)] * 3,
        out_specs=pl.BlockSpec(memory_space=pl.ANY),
        scratch_shapes=[
            pltpu.VMEM((2, groups, blocks, lanes), jnp.float32),
            pltpu.VMEM((2, groups, blocks, lanes), jnp.float32),
            pltpu.VMEM((blocks, 2 * length, columns), jnp.bfloat16),
            pltpu.VMEM((blocks + 1, half, columns), jnp.float32),
            pltpu.SemaphoreType.DMA((blocks + 1,)),
        ],
        compiler_params=pltpu.CompilerParams(vmem_limit_bytes=VMEM_LIMIT),
        cost_estimate=pl.CostEstimate(
            flops=4 * length * length * blocks * columns,
            transcendentals=0,
            bytes_accessed=4 * (blocks + 1) * half * columns,
        ),
        name="synthesize",
    )(coefficients, moved_modes, table)


def sum_over_space(partial):
    count = lax.axis_size("space")
    chips = count // 2

    def beside(value):
        return lax.ppermute(value, "space", [(i, i ^ 1) for i in range(count)])

    def around(value, hops):
        pairs = [(2 * z, 2 * ((z + hops) % chips)) for z in range(chips)]
        if 2 * hops != chips:
            pairs += [(2 * z + 1, 2 * ((z - hops) % chips) + 1) for z in range(chips)]
        return lax.ppermute(value, "space", pairs)

    chip = partial + beside(partial)
    arrived = sum(around(chip, hops) for hops in range(1, chips // 2 + 1))
    return chip + arrived + beside(arrived)


def body(spectra, eigvecs, weights):
    points_dev = spectra.shape[3]
    groups = lax.axis_size("freq")
    factor = 1.0 / math.sqrt(points_dev * lax.axis_size("space"))
    pieces = cut_points(eigvecs, groups)
    moved = lax.all_to_all(pieces, "freq", split_axis=0, concat_axis=0, tiled=True)
    same_eigvecs, _ = lax.optimization_barrier((eigvecs, pieces))
    coefficients = sum_over_space(project(spectra, same_eigvecs, weights, 4)) * factor
    coefficients, moved = lax.optimization_barrier((coefficients, moved))
    copies = jnp.broadcast_to(coefficients, (groups, *coefficients.shape))
    gathered = lax.all_to_all(copies, "freq", split_axis=0, concat_axis=0, tiled=True)
    length = groups * spectra.shape[1]
    filtered = synthesize(
        gathered,
        moved.reshape(groups, -1, moved.shape[-1]),
        transform_table(length, groups),
    )
    return filtered.reshape(-1, filtered.shape[-1])


def solution(mesh):
    placed = (P(None, "freq", None, "space"), P(None, "freq", None, "space"), P("space"))
    return jax.shard_map(
        body, mesh=mesh, in_specs=placed, out_specs=P(None, ("space", "freq")), check_vma=False
    )
```

profile of v0, /device:TPU:1, one launch (start us, length us, event | category | flops | bytes accessed | tf_op | source)
XLA Modules:
  0.0 87.1 jit_solution(5012927085101734039)
XLA Ops:
  0.0 33.0 %cut_points.1 = bf16[16,2,16,4,256]{4,3,2,1,0:T(4,128)(2,1)} custom-call(bf16[2,16,4,4096]{3,2,1,0:T(4,128)(2,1)} %eigvecs_ref), custom_call_target="tpu_custom_call" | custom-call | bytes 2097152 | tf_op jit(solution)/shard_map/cut_points/pallas_call | solution.py:27
  33.0 0.0 copy-start.1
  33.0 7.7 %all-to-all-start = ((bf16[16,2,16,4,256]{4,3,2,1,0:T(4,128)(2,1)}), bf16[16,2,16,4,256]{4,3,2,1,0:T(4,128)(2,1)S(1)}, u32[]{:S(2)}, u32[]{:S(2)}) async-start(bf16[16,2,16,4,256]{4,3,2,1,0:T(4,128)(2,1)} %cut_points.1), calls=%async_computation | async-start | bytes 2097152 | tf_op jit(solution)/shard_map/all_to_all | solution.py:220
  40.8 0.7 reshape.9.weights_ref
  41.5 0.0 copy-start
  41.5 1.2 %copy-done = bf16[2,16,4,4096]{3,2,1,0:T(4,128)(2,1)S(1)} copy-done((bf16[2,16,4,4096]{3,2,1,0:T(4,128)(2,1)S(1)}, bf16[2,16,4,4096]{3,2,1,0:T(4,128)(2,1)}, u32[]{:S(2)}) %copy-start) | copy-done | bytes 1048600
  42.7 5.1 %project.1 = f32[24,128]{1,0:T(8,128)S(1)} custom-call(bf16[2,16,24,4096]{3,2,1,0:T(8,128)(2,1)} %spectra_ref.1, bf16[2,16,4,4096]{3,2,1,0:T(4,128)(2,1)S(1)} %copy-done, bf16[1,4096]{1,0:T(2,128)(2,1)S(1)} %reshape.9.weights_ref), custom_call_target="tpu_custom_call" | custom-call | flops 50331648 | bytes 7340032 | tf_op jit(solution)/shard_map/project/pallas_call | solution.py:87
  47.8 1.0 %collective-permute-start = (f32[24,128]{1,0:T(8,128)S(1)}, f32[24,128]{1,0:T(8,128)S(1)}, u32[]{:S(2)}, u32[]{:S(2)}) collective-permute-start(f32[24,128]{1,0:T(8,128)S(1)} %project.1), channel_id=1, source_target_pairs={{0,1},{1,0},{2,3},{3,2},{4,5},{5,4},{6,7},{7,6},{8,9},{9,8},{10,11... | collective-permute-start | bytes 36872 | tf_op jit(solution)/shard_map/ppermute | solution.py:202
  48.9 0.8 collective-permute-done
  49.7 0.7 collective-permute-start.4
  50.4 6.5 %collective-permute-start.3 = (f32[24,128]{1,0:T(8,128)S(1)}, f32[24,128]{1,0:T(8,128)S(1)}, u32[]{:S(2)}, u32[]{:S(2)}) collective-permute-start(f32[24,128]{1,0:T(8,128)S(1)} %add.18), channel_id=1, source_target_pairs={{0,6},{2,8},{4,10},{6,12},{8,14},{10,0},{12,2},{14,4},{1,11},{3,13... | collective-permute-start | bytes 36872 | tf_op jit(solution)/shard_map/ppermute | solution.py:208
  56.9 0.3 collective-permute-start.2
  57.2 0.5 collective-permute-start.1
  57.7 0.0 collective-permute-done.4
  57.7 0.1 collective-permute-done.3
  57.8 2.7 %collective-permute-done.2 = f32[24,128]{1,0:T(8,128)S(1)} collective-permute-done((f32[24,128]{1,0:T(8,128)S(1)}, f32[24,128]{1,0:T(8,128)S(1)}, u32[]{:S(2)}, u32[]{:S(2)}) %collective-permute-start.2) | collective-permute-done | bytes 12320 | tf_op jit(solution)/shard_map/ppermute | solution.py:208
  60.4 0.0 collective-permute-done.1
  60.4 6.6 %collective-permute-start.5 = (f32[24,128]{1,0:T(8,128)S(1)}, f32[24,128]{1,0:T(8,128)S(1)}, u32[]{:S(2)}, u32[]{:S(2)}) collective-permute-start(f32[24,128]{1,0:T(8,128)S(1)} %add_add_fusion), channel_id=1, source_target_pairs={{0,1},{1,0},{2,3},{3,2},{4,5},{5,4},{6,7},{7,6},{8,9},{9,8},{10,11... | collective-permute-start | bytes 36872 | tf_op jit(solution)/shard_map/ppermute | solution.py:202
  67.1 0.8 collective-permute-done.5
  67.9 0.0 all-to-all-done
  67.9 0.7 broadcast_in_dim.3
  68.6 6.9 %all-to-all-start.1 = ((f32[16,24,128]{2,1,0:T(8,128)}), f32[16,24,128]{2,1,0:T(8,128)S(1)}, u32[]{:S(2)}, u32[]{:S(2)}) async-start(f32[16,24,128]{2,1,0:T(8,128)} %broadcast_in_dim.3), calls=%async_computation.1 | async-start | bytes 393216 | tf_op jit(solution)/shard_map/all_to_all | solution.py:225
  75.6 0.3 reshape.10.modes_ref
  75.8 6.7 %all-to-all-done.1.coef_ref = f32[16,24,128]{2,1,0:T(8,128)S(1)} async-done(((f32[16,24,128]{2,1,0:T(8,128)}), f32[16,24,128]{2,1,0:T(8,128)S(1)}, u32[]{:S(2)}, u32[]{:S(2)}) %all-to-all-start.1) | async-done | bytes 196640 | tf_op jit(solution)/shard_map/all_to_all | solution.py:225
  82.6 0.0 copy-done.1
  82.6 4.5 %synthesize.1 = f32[25,128,256]{2,1,0:T(8,128)} custom-call(f32[16,24,128]{2,1,0:T(8,128)S(1)} %all-to-all-done.1.coef_ref, bf16[16,128,256]{2,1,0:T(8,128)(2,1)S(1)} %reshape.10.modes_ref, bf16[256,512]{1,0:T(8,128)(2,1)S(1)} %copy-done.1), custom_call_target="tpu_custom_call" | custom-call | flops 1610612736 | bytes 3276800 | tf_op jit(solution)/shard_map/synthesize/pallas_call | solution.py:175
  (3 shorter events, 0.0 us)
Async XLA Ops:
  33.0 49.6 %copy-start.1 = (bf16[256,512]{1,0:T(8,128)(2,1)S(1)}, bf16[256,512]{1,0:T(8,128)(2,1)}, u32[]{:S(2)}) copy-start(bf16[256,512]{1,0:T(8,128)(2,1)} %constant.4.clone.table_ref) | copy-start | bytes 786436
  33.0 34.9 %all-to-all-start = ((bf16[16,2,16,4,256]{4,3,2,1,0:T(4,128)(2,1)}), bf16[16,2,16,4,256]{4,3,2,1,0:T(4,128)(2,1)S(1)}, u32[]{:S(2)}, u32[]{:S(2)}) async-start(bf16[16,2,16,4,256]{4,3,2,1,0:T(4,128)(2,1)} %cut_points.1), calls=%async_computation | async-start | bytes 2097152 | tf_op jit(solution)/shard_map/all_to_all | solution.py:220
  41.5 1.2 %copy-start = (bf16[2,16,4,4096]{3,2,1,0:T(4,128)(2,1)S(1)}, bf16[2,16,4,4096]{3,2,1,0:T(4,128)(2,1)}, u32[]{:S(2)}) copy-start(bf16[2,16,4,4096]{3,2,1,0:T(4,128)(2,1)} %eigvecs_ref) | copy-start | bytes 3145732
  47.8 1.9 %collective-permute-start = (f32[24,128]{1,0:T(8,128)S(1)}, f32[24,128]{1,0:T(8,128)S(1)}, u32[]{:S(2)}, u32[]{:S(2)}) collective-permute-start(f32[24,128]{1,0:T(8,128)S(1)} %project.1), channel_id=1, source_target_pairs={{0,1},{1,0},{2,3},{3,2},{4,5},{5,4},{6,7},{7,6},{8,9},{9,8},{10,11... | collective-permute-start | bytes 36872 | tf_op jit(solution)/shard_map/ppermute | solution.py:202
  49.7 7.9 %collective-permute-start.4 = (f32[24,128]{1,0:T(8,128)S(1)}, f32[24,128]{1,0:T(8,128)S(1)}, u32[]{:S(2)}, u32[]{:S(2)}) collective-permute-start(f32[24,128]{1,0:T(8,128)S(1)} %add.18), channel_id=1, source_target_pairs={{0,8},{2,10},{4,12},{6,14},{8,0},{10,2},{12,4},{14,6},{16,24},{18,... | collective-permute-start | bytes 36872 | tf_op jit(solution)/shard_map/ppermute | solution.py:208
  50.4 7.4 %collective-permute-start.3 = (f32[24,128]{1,0:T(8,128)S(1)}, f32[24,128]{1,0:T(8,128)S(1)}, u32[]{:S(2)}, u32[]{:S(2)}) collective-permute-start(f32[24,128]{1,0:T(8,128)S(1)} %add.18), channel_id=1, source_target_pairs={{0,6},{2,8},{4,10},{6,12},{8,14},{10,0},{12,2},{14,4},{1,11},{3,13... | collective-permute-start | bytes 36872 | tf_op jit(solution)/shard_map/ppermute | solution.py:208
  56.9 3.5 %collective-permute-start.2 = (f32[24,128]{1,0:T(8,128)S(1)}, f32[24,128]{1,0:T(8,128)S(1)}, u32[]{:S(2)}, u32[]{:S(2)}) collective-permute-start(f32[24,128]{1,0:T(8,128)S(1)} %add.18), channel_id=1, source_target_pairs={{0,4},{2,6},{4,8},{6,10},{8,12},{10,14},{12,0},{14,2},{1,13},{3,15... | collective-permute-start | bytes 36872 | tf_op jit(solution)/shard_map/ppermute | solution.py:208
  57.2 3.2 %collective-permute-start.1 = (f32[24,128]{1,0:T(8,128)S(1)}, f32[24,128]{1,0:T(8,128)S(1)}, u32[]{:S(2)}, u32[]{:S(2)}) collective-permute-start(f32[24,128]{1,0:T(8,128)S(1)} %add.18), channel_id=1, source_target_pairs={{0,2},{2,4},{4,6},{6,8},{8,10},{10,12},{12,14},{14,0},{1,15},{3,1}... | collective-permute-start | bytes 36872 | tf_op jit(solution)/shard_map/ppermute | solution.py:208
  60.4 7.5 %collective-permute-start.5 = (f32[24,128]{1,0:T(8,128)S(1)}, f32[24,128]{1,0:T(8,128)S(1)}, u32[]{:S(2)}, u32[]{:S(2)}) collective-permute-start(f32[24,128]{1,0:T(8,128)S(1)} %add_add_fusion), channel_id=1, source_target_pairs={{0,1},{1,0},{2,3},{3,2},{4,5},{5,4},{6,7},{7,6},{8,9},{9,8},{10,11... | collective-permute-start | bytes 36872 | tf_op jit(solution)/shard_map/ppermute | solution.py:202
  68.6 14.0 %all-to-all-start.1 = ((f32[16,24,128]{2,1,0:T(8,128)}), f32[16,24,128]{2,1,0:T(8,128)S(1)}, u32[]{:S(2)}, u32[]{:S(2)}) async-start(f32[16,24,128]{2,1,0:T(8,128)} %broadcast_in_dim.3), calls=%async_computation.1 | async-start | bytes 393216 | tf_op jit(solution)/shard_map/all_to_all | solution.py:225
where the time goes:
time: 87.5 us; the launch traced here: 87.1 us
  Pallas kernels  42.7 us (49%)
  starting transfers between devices  30.3 us (35%)
  waiting for transfers between devices  11.2 us (13%)
  local copies, waits for them, and re-layouts  2.91 us (3%)
    pallas_call x1, Pallas kernels, cut_points(): pl.pallas_call(kernel, out_shape=jax.ShapeDtypeStruct((parts, *eigvecs.sh...  33 us
    ppermute x4, starting transfers between devices, around(): return lax.ppermute(value, 'space', pairs)  7.92 us
    all_to_all x1, starting transfers between devices, body(): lax.all_to_all(pieces, 'freq', split_axis=0, concat_axis=0, tiled=True)  7.73 us
    ppermute x2, starting transfers between devices, beside(): return lax.ppermute(value, 'space', [(i, i ^ 1) for i in range(count)])  7.67 us
    all_to_all x1, starting transfers between devices, body(): lax.all_to_all(copies, 'freq', split_axis=0, concat_axis=0, tiled=True)  6.94 us
    all_to_all x1, waiting for transfers between devices, body(): lax.all_to_all(copies, 'freq', split_axis=0, concat_axis=0, tiled=True)  6.74 us
    pallas_call x1, Pallas kernels, project(): pl.pallas_call(kernel, grid=(steps,), out_shape=jax.ShapeDtypeStruct((blo...  5.14 us
    pallas_call x1, Pallas kernels, synthesize(): pl.pallas_call(kernel, out_shape=jax.ShapeDtypeStruct((blocks + 1, half,...  4.51 us
  transfers between devices with their start and end apart: 8, of which 5 were waited for; matrix products, arithmetic and copies ran while one was open for 1% of the time, Pallas kernels for 6%

commit v1 on v0

v1 whole, which is shorter than its diff:
```python
import math

import jax
import jax.numpy as jnp
import numpy as np
from jax import lax
from jax.experimental import pallas as pl
from jax.experimental.pallas import tpu as pltpu
from jax.sharding import PartitionSpec as P

MIB = 1024 * 1024
LANES = 128


def project(spectra, eigvecs, weights, copies):
    _, freqs, blocks, points = spectra.shape
    modes = eigvecs.shape[2]
    half = freqs * modes
    rows = 2 * freqs * blocks
    ends = [rows // 4, rows // 2, rows * 3 // 4, rows * 7 // 8, rows]
    starts = [0, *ends[:-1]]
    dtype = spectra.dtype

    def kernel(
        spectra_hbm, eigvecs_hbm, weights_hbm, out_ref,
        spectra_ref, eigvecs_ref, weights_ref, weighted, columns, total, done,
    ):
        small = pltpu.make_async_copy(weights_hbm, weights_ref, done.at[0])
        small.start()
        by_part = [
            pltpu.make_async_copy(eigvecs_hbm.at[part], eigvecs_ref.at[part], done.at[1 + part])
            for part in range(2)
        ]
        for copy in by_part:
            copy.start()
        by_rows = []
        for i, (start, end) in enumerate(zip(starts, ends)):
            some = pl.ds(start, end - start)
            by_rows.append(
                pltpu.make_async_copy(spectra_hbm.at[some], spectra_ref.at[some], done.at[3 + i])
            )
            by_rows[-1].start()
        small.wait()
        per_row = weights_ref[...].astype(jnp.float32)
        scale = jnp.concatenate([per_row[i : i + 1] for i in range(points // LANES)], axis=1)
        for part in range(2):
            by_part[part].wait()
            for k in range(freqs):
                first = part * half + k * modes
                weighted[first : first + modes] = (
                    eigvecs_ref[part, k].astype(jnp.float32) * scale
                )
        columns[...] = jnp.transpose(weighted[...]).astype(dtype)
        for copy, start, end in zip(by_rows, starts, ends):
            copy.wait()
            total[start:end] = jnp.dot(
                spectra_ref[start:end], columns[...], preferred_element_type=jnp.float32
            )
        lane = lax.broadcasted_iota(jnp.int32, (blocks, 2 * half), 1)
        sums = []
        for part in range(2):
            kept = jnp.zeros((blocks, 2 * half), jnp.float32)
            for k in range(freqs):
                first = (part * freqs + k) * blocks
                own = (lane % half) // modes == k
                kept = jnp.where(own, total[first : first + blocks], kept)
            sums.append(kept)
        value = jnp.where(lane < half, sums[0], -sums[0]) + pltpu.roll(sums[1], half, 1)
        for copy in range(copies):
            out_ref[copy] = value

    return pl.pallas_call(
        kernel,
        out_shape=jax.ShapeDtypeStruct((copies, blocks, 2 * half), jnp.float32),
        in_specs=[pl.BlockSpec(memory_space=pl.ANY)] * 3,
        out_specs=pl.BlockSpec(memory_space=pltpu.VMEM),
        scratch_shapes=[
            pltpu.VMEM((rows, points), dtype),
            pltpu.VMEM(eigvecs.shape, dtype),
            pltpu.VMEM((points // LANES, LANES), dtype),
            pltpu.VMEM((2 * half, points), jnp.float32),
            pltpu.VMEM((points, 2 * half), dtype),
            pltpu.VMEM((rows, 2 * half), jnp.float32),
            pltpu.SemaphoreType.DMA((3 + len(ends),)),
        ],
        compiler_params=pltpu.CompilerParams(vmem_limit_bytes=60 * MIB),
        cost_estimate=pl.CostEstimate(
            flops=8 * freqs * blocks * modes * points,
            transcendentals=0,
            bytes_accessed=2 * (spectra.size + eigvecs.size),
        ),
        name="project",
    )(spectra.reshape(rows, points), eigvecs, weights.reshape(points // LANES, LANES))


def cut_points(eigvecs, parts, spare):
    kinds, freqs, modes, points = eigvecs.shape
    width = points // parts
    rows = kinds * freqs * modes
    shape = (parts, rows + spare, width)

    def kernel(source, pieces, staged, done):
        copies = []
        for part in range(parts):
            for kind in range(kinds):
                for k in range(freqs):
                    first = (kind * freqs + k) * modes
                    staged[part, first : first + modes] = source[
                        kind, k, :, part * width : (part + 1) * width
                    ]
            copies.append(
                pltpu.make_async_copy(
                    staged.at[part], pieces.at[part, pl.ds(0, rows)], done.at[part]
                )
            )
            copies[-1].start()
        for copy in copies:
            copy.wait()

    return pl.pallas_call(
        kernel,
        out_shape=jax.ShapeDtypeStruct(shape, eigvecs.dtype),
        in_specs=[pl.BlockSpec(memory_space=pltpu.VMEM)],
        out_specs=pl.BlockSpec(memory_space=pl.ANY),
        scratch_shapes=[
            pltpu.VMEM((parts, rows, width), eigvecs.dtype),
            pltpu.SemaphoreType.DMA((parts,)),
        ],
        compiler_params=pltpu.CompilerParams(vmem_limit_bytes=8 * MIB),
        cost_estimate=pl.CostEstimate(
            flops=0, transcendentals=0, bytes_accessed=2 * eigvecs.size * eigvecs.dtype.itemsize
        ),
        name="cut_points",
    )(eigvecs)


def add_coefficients(terms, pieces, factor):
    _, blocks, lanes = terms.shape
    parts, rows, _ = pieces.shape

    def kernel(terms_ref, _, out_ref, staged, done):
        value = terms_ref[0]
        for i in range(1, terms.shape[0]):
            value += terms_ref[i]
        value *= factor
        high = value.astype(jnp.bfloat16)
        staged[:, :lanes] = high
        staged[:, lanes:] = (value - high.astype(jnp.float32)).astype(jnp.bfloat16)
        copies = [
            pltpu.make_async_copy(
                staged, out_ref.at[part, pl.ds(rows - blocks, blocks)], done.at[part]
            )
            for part in range(parts)
        ]
        for copy in copies:
            copy.start()
        for copy in copies:
            copy.wait()

    return pl.pallas_call(
        kernel,
        out_shape=jax.ShapeDtypeStruct(pieces.shape, pieces.dtype),
        in_specs=[pl.BlockSpec(memory_space=pltpu.VMEM), pl.BlockSpec(memory_space=pl.ANY)],
        out_specs=pl.BlockSpec(memory_space=pl.ANY),
        scratch_shapes=[
            pltpu.VMEM((blocks, 2 * lanes), pieces.dtype),
            pltpu.SemaphoreType.DMA((parts,)),
        ],
        input_output_aliases={1: 0},
        compiler_params=pltpu.CompilerParams(vmem_limit_bytes=4 * MIB),
        cost_estimate=pl.CostEstimate(
            flops=terms.size, transcendentals=0, bytes_accessed=4 * terms.size
        ),
        name="add_coefficients",
    )(terms, pieces)


def transform_table(length, groups):
    sample = np.arange(length)
    phase = 2.0 * np.pi * ((sample[:, None] * sample[None, :]) % length) / length
    window = np.sin(np.pi * (sample + 0.5) / length) / math.sqrt(length)
    table = np.stack([np.cos(phase), -np.sin(phase)], axis=1) * window[:, None, None]
    table = table.reshape(length, 2, groups, length // groups).transpose(0, 2, 1, 3)
    return jnp.asarray(table.reshape(length, 2 * length), jnp.bfloat16)


def synthesize(pieces, table, blocks):
    groups, rows, columns = pieces.shape
    lanes = rows - blocks
    length = table.shape[0]
    freqs = length // groups
    modes = lanes // (2 * freqs)
    half_lanes = lanes // 2
    half = length // 2

    def kernel(pieces_ref, table_ref, out_ref, high, low, rebuilt, result, done):
        lane = lax.broadcasted_iota(jnp.int32, (freqs, lanes), 1)
        row = lax.broadcasted_iota(jnp.int32, (freqs, lanes), 0)
        own = jnp.where((lane % half_lanes) // modes == row, 1.0, 0.0)
        signed = jnp.where(lane < half_lanes, own, -own)
        for group in range(groups):
            both = pieces_ref[group, lanes:].astype(jnp.float32)
            for side, value in ((high, both[:, :lanes]), (low, both[:, lanes:])):
                side[0, group] = value
                side[1, group] = pltpu.roll(value, half_lanes, 1)
        for group in range(groups):
            tiles = []
            for block in range(blocks):
                for kind, mask in enumerate((signed, own)):
                    tiles.append(
                        jnp.concatenate(
                            [
                                (jnp.broadcast_to(
                                    side[kind, group, pl.ds(block, 1), :], (freqs, lanes)
                                ) * mask).astype(jnp.bfloat16)
                                for side in (high, low)
                            ],
                            axis=1,
                        )
                    )
            values = pieces_ref[group, :lanes]
            product = jnp.dot(
                jnp.concatenate(tiles, axis=0),
                jnp.concatenate([values, values], axis=0),
                preferred_element_type=jnp.float32,
            )
            rebuilt[:, group * 2 * freqs : (group + 1) * 2 * freqs, :] = product.astype(
                jnp.bfloat16
            ).reshape(blocks, 2 * freqs, columns)
        result[0] = jnp.zeros((half, columns), jnp.float32)

        def send(block):
            return pltpu.make_async_copy(result.at[block], out_ref.at[block], done.at[block])

        for block in range(blocks):
            series = jnp.dot(table_ref[...], rebuilt[block], preferred_element_type=jnp.float32)
            result[block] += series[:half]
            result[block + 1] = series[half:]
            send(block).start()
        send(blocks).start()
        for block in range(blocks + 1):
            send(block).wait()

    return pl.pallas_call(
        kernel,
        out_shape=jax.ShapeDtypeStruct((blocks + 1, half, columns), jnp.float32),
        in_specs=[pl.BlockSpec(memory_space=pltpu.VMEM)] * 2,
        out_specs=pl.BlockSpec(memory_space=pl.ANY),
        scratch_shapes=[
            pltpu.VMEM((2, groups, blocks, lanes), jnp.float32),
            pltpu.VMEM((2, groups, blocks, lanes), jnp.float32),
            pltpu.VMEM((blocks, 2 * length, columns), jnp.bfloat16),
            pltpu.VMEM((blocks + 1, half, columns), jnp.float32),
            pltpu.SemaphoreType.DMA((blocks + 1,)),
        ],
        compiler_params=pltpu.CompilerParams(vmem_limit_bytes=32 * MIB),
        cost_estimate=pl.CostEstimate(
            flops=4 * length * length * blocks * columns,
            transcendentals=0,
            bytes_accessed=4 * (blocks + 1) * half * columns,
        ),
        name="synthesize",
    )(pieces, table)


def body(spectra, eigvecs, weights):
    _, freqs, blocks, points_dev = spectra.shape
    groups = lax.axis_size("freq")
    along_space = lax.axis_size("space")
    factor = 1.0 / math.sqrt(points_dev * along_space)
    partial = project(spectra, eigvecs, weights, along_space)
    terms = lax.all_to_all(partial, "space", split_axis=0, concat_axis=0, tiled=True)
    later_eigvecs, _ = lax.optimization_barrier((eigvecs, partial))
    pieces = add_coefficients(terms, cut_points(later_eigvecs, groups, blocks), factor)
    moved = lax.all_to_all(pieces, "freq", split_axis=0, concat_axis=0, tiled=True)
    filtered = synthesize(moved, transform_table(groups * freqs, groups), blocks)
    return filtered.reshape(-1, filtered.shape[-1])


def solution(mesh):
    placed = (P(None, "freq", None, "space"), P(None, "freq", None, "space"), P("space"))
    return jax.shard_map(
        body, mesh=mesh, in_specs=placed, out_specs=P(None, ("space", "freq")), check_vma=False
    )
```

time: 87.5 us -> 56.2 us (0.64)
  Pallas kernels: 42.7 us -> 11.9 us
  blocking collectives: 0 us -> 25.5 us
  starting transfers between devices: 30.3 us -> 10 us
  local copies, waits for them, and re-layouts: 2.91 us -> 0.01 us
  waiting for transfers between devices: 11.2 us -> 8.44 us
    pallas_call x2 -> x3, Pallas kernels: 38.1 us -> 7.38 us  [the longest x1 5.06 us: project(): pl.pallas_call(kernel, out_shape=jax.ShapeDtypeStruct((copies, blocks, 2...]
    all_to_all x0 -> x1, blocking collectives: none -> 25.5 us  [body(): lax.all_to_all(pieces, 'freq', split_axis=0, concat_axis=0, tiled=True)]
    ppermute x6 -> x0, starting transfers between devices: 15.6 us -> none  [the longest x4 7.92 us: around(): return lax.ppermute(value, 'space', pairs)]
    all_to_all x2 -> x1, starting transfers between devices: 14.7 us -> 10 us  [body(): lax.all_to_all(partial, 'space', split_axis=0, concat_axis=0, tiled=True)]
    ppermute x6 -> x0, waiting for transfers between devices: 4.44 us -> none  [the longest x4 2.77 us: around(): return lax.ppermute(value, 'space', pairs)]
    all_to_all x2 -> x1, waiting for transfers between devices: 6.74 us -> 8.44 us  [body(): lax.all_to_all(partial, 'space', split_axis=0, concat_axis=0, tiled=True)]
    unnamed x4, local copies, waits for them, and re-layouts: 1.23 us -> 0.01 us
    reshape x2 -> x0, local copies, waits for them, and re-layouts: 1 us -> none  [the longest x1 0.71 us: project(): weights.reshape(1, points)]
  transfers between devices with their start and end apart: 8 -> 1, of which waited for: 5 -> 1; matrix products, arithmetic and copies ran while one was open for 1% -> 0% of each run, Pallas kernels for 6% -> 3%
where the time goes in v1:
time: 56.2 us; the launch traced here: 55.9 us
  blocking collectives  25.5 us (45%)
  Pallas kernels  11.9 us (21%)
  starting transfers between devices  10 us (18%)
  waiting for transfers between devices  8.44 us (15%)
    all_to_all x1, blocking collectives, body(): lax.all_to_all(pieces, 'freq', split_axis=0, concat_axis=0, tiled=True)  25.5 us
    all_to_all x1, starting transfers between devices, body(): lax.all_to_all(partial, 'space', split_axis=0, concat_axis=0, tiled=True)  10 us
    all_to_all x1, waiting for transfers between devices, body(): lax.all_to_all(partial, 'space', split_axis=0, concat_axis=0, tiled=True)  8.44 us
    pallas_call x1, Pallas kernels, project(): pl.pallas_call(kernel, out_shape=jax.ShapeDtypeStruct((copies, blocks, 2...  5.06 us
    pallas_call x1, Pallas kernels, synthesize(): pl.pallas_call(kernel, out_shape=jax.ShapeDtypeStruct((blocks + 1, half,...  4.53 us
    pallas_call x1, Pallas kernels, cut_points(): pl.pallas_call(kernel, out_shape=jax.ShapeDtypeStruct(shape, eigvecs.dtyp...  1.87 us
  transfers between devices with their start and end apart: 1, of which 1 were waited for; matrix products, arithmetic and copies ran while one was open for 0% of the time, Pallas kernels for 3%

profile of v1, /device:TPU:1, one launch (start us, length us, event | category | flops | bytes accessed | tf_op | source)
XLA Modules:
  0.0 55.9 jit_solution(2370234343556058448)
XLA Ops:
  0.0 0.0 copy-start
  0.0 5.1 %project.1 = f32[16,24,128]{2,1,0:T(8,128)} custom-call(bf16[768,4096]{1,0:T(8,128)(2,1)} %bitcast.3, bf16[2,16,4,4096]{3,2,1,0:T(4,128)(2,1)} %source, bf16[32,128]{1,0:T(8,128)(2,1)} %bitcast.4), custom_call_target="tpu_custom_call" | custom-call | flops 50331648 | bytes 7340032 | tf_op jit(solution)/shard_map/project/pallas_call | solution.py:72
  5.1 10.0 %all-to-all-start = ((f32[16,24,128]{2,1,0:T(8,128)}), f32[16,24,128]{2,1,0:T(8,128)S(1)}, u32[]{:S(2)}, u32[]{:S(2)}) async-start(f32[16,24,128]{2,1,0:T(8,128)} %project.1), calls=%async_computation | async-start | bytes 393216 | tf_op jit(solution)/shard_map/all_to_all | solution.py:272
  15.1 0.0 copy-done
  15.1 1.9 %cut_points.1._ = bf16[16,152,256]{2,1,0:T(8,128)(2,1)S(1)} custom-call(bf16[2,16,4,4096]{3,2,1,0:T(4,128)(2,1)S(1)} %copy-done), custom_call_target="tpu_custom_call" | custom-call | bytes 2097152 | tf_op jit(solution)/shard_map/cut_points/pallas_call | solution.py:120
  17.0 8.4 %all-to-all-done.terms_ref = f32[16,24,128]{2,1,0:T(8,128)S(1)} async-done(((f32[16,24,128]{2,1,0:T(8,128)}), f32[16,24,128]{2,1,0:T(8,128)S(1)}, u32[]{:S(2)}, u32[]{:S(2)}) %all-to-all-start) | async-done | bytes 196640 | tf_op jit(solution)/shard_map/all_to_all | solution.py:272
  25.4 0.4 add_coefficients.1
  25.9 0.0 copy-start.1
  25.9 25.5 %all_to_all.10.pieces_ref = bf16[16,152,256]{2,1,0:T(8,128)(2,1)S(1)} all-to-all(bf16[16,152,256]{2,1,0:T(8,128)(2,1)S(1)} %add_coefficients.1), channel_id=1, replica_groups=mesh['freq'=16,'space'=16] {'freq'}, dimensions={0} | all-to-all | bytes 2490368 | tf_op jit(solution)/shard_map/all_to_all | solution.py:275
  51.4 0.0 copy-done.1
  51.4 4.5 %synthesize.1 = f32[25,128,256]{2,1,0:T(8,128)} custom-call(bf16[16,152,256]{2,1,0:T(8,128)(2,1)S(1)} %all_to_all.10.pieces_ref, bf16[256,512]{1,0:T(8,128)(2,1)S(1)} %copy-done.1), custom_call_target="tpu_custom_call" | custom-call | flops 1610612736 | bytes 3276800 | tf_op jit(solution)/shard_map/synthesize/pallas_call | solution.py:244
Async XLA Ops:
  0.0 15.1 %copy-start = (bf16[2,16,4,4096]{3,2,1,0:T(4,128)(2,1)S(1)}, bf16[2,16,4,4096]{3,2,1,0:T(4,128)(2,1)}, u32[]{:S(2)}) copy-start(bf16[2,16,4,4096]{3,2,1,0:T(4,128)(2,1)} %source) | copy-start | bytes 3145732
  5.1 20.3 %all-to-all-start = ((f32[16,24,128]{2,1,0:T(8,128)}), f32[16,24,128]{2,1,0:T(8,128)S(1)}, u32[]{:S(2)}, u32[]{:S(2)}) async-start(f32[16,24,128]{2,1,0:T(8,128)} %project.1), calls=%async_computation | async-start | bytes 393216 | tf_op jit(solution)/shard_map/all_to_all | solution.py:272
  25.9 25.6 %copy-start.1 = (bf16[256,512]{1,0:T(8,128)(2,1)S(1)}, bf16[256,512]{1,0:T(8,128)(2,1)}, u32[]{:S(2)}) copy-start(bf16[256,512]{1,0:T(8,128)(2,1)} %constant.2.clone.table_ref) | copy-start | bytes 786436

commit v2 on v1

v2 whole, which is shorter than its diff:
```python
import math

import jax
import jax.numpy as jnp
import numpy as np
from jax import lax
from jax.experimental import pallas as pl
from jax.experimental.pallas import tpu as pltpu
from jax.sharding import PartitionSpec as P

MIB = 1024 * 1024
LANES = 128


def project(spectra, eigvecs, weights, parts):
    _, freqs, blocks, points = spectra.shape
    modes = eigvecs.shape[2]
    half = freqs * modes
    rows = 2 * freqs * blocks
    width = points // parts
    ends = [rows // 4, rows // 2, rows * 3 // 4, rows * 7 // 8, rows]
    starts = [0, *ends[:-1]]
    dtype = spectra.dtype

    def kernel(
        spectra_hbm, eigvecs_hbm, weights_hbm, out_ref, pieces_ref,
        spectra_ref, eigvecs_ref, weights_ref, weighted, columns, total, done,
    ):
        small = pltpu.make_async_copy(weights_hbm, weights_ref, done.at[0])
        small.start()
        by_part = [
            pltpu.make_async_copy(eigvecs_hbm.at[part], eigvecs_ref.at[part], done.at[1 + part])
            for part in range(2)
        ]
        for copy in by_part:
            copy.start()
        by_rows = []
        for i, (start, end) in enumerate(zip(starts, ends)):
            some = pl.ds(start, end - start)
            by_rows.append(
                pltpu.make_async_copy(spectra_hbm.at[some], spectra_ref.at[some], done.at[3 + i])
            )
            by_rows[-1].start()
        small.wait()
        per_row = weights_ref[...].astype(jnp.float32)
        scale = jnp.concatenate([per_row[i : i + 1] for i in range(points // LANES)], axis=1)
        for part in range(2):
            by_part[part].wait()
            for k in range(freqs):
                first = part * half + k * modes
                weighted[first : first + modes] = (
                    eigvecs_ref[part, k].astype(jnp.float32) * scale
                )
        columns[...] = jnp.transpose(weighted[...]).astype(dtype)
        for piece in range(parts):
            pieces_ref[piece] = eigvecs_ref[:, :, :, piece * width : (piece + 1) * width]
        for copy, start, end in zip(by_rows, starts, ends):
            copy.wait()
            total[start:end] = jnp.dot(
                spectra_ref[start:end], columns[...], preferred_element_type=jnp.float32
            )
        lane = lax.broadcasted_iota(jnp.int32, (blocks, 2 * half), 1)
        sums = []
        for part in range(2):
            kept = jnp.zeros((blocks, 2 * half), jnp.float32)
            for k in range(freqs):
                first = (part * freqs + k) * blocks
                own = (lane % half) // modes == k
                kept = jnp.where(own, total[first : first + blocks], kept)
            sums.append(kept)
        out_ref[...] = jnp.where(lane < half, sums[0], -sums[0]) + pltpu.roll(sums[1], half, 1)

    operands = (
        spectra.reshape(rows, points), eigvecs, weights.reshape(points // LANES, LANES)
    )
    return pl.pallas_call(
        kernel,
        out_shape=[
            jax.ShapeDtypeStruct((blocks, 2 * half), jnp.float32),
            jax.ShapeDtypeStruct((parts, 2, freqs, modes, width), dtype),
        ],
        in_specs=[pl.BlockSpec(memory_space=pl.ANY)] * 3,
        out_specs=[pl.BlockSpec(memory_space=pltpu.VMEM)] * 2,
        scratch_shapes=[
            pltpu.VMEM((rows, points), dtype),
            pltpu.VMEM(eigvecs.shape, dtype),
            pltpu.VMEM((points // LANES, LANES), dtype),
            pltpu.VMEM((2 * half, points), jnp.float32),
            pltpu.VMEM((points, 2 * half), dtype),
            pltpu.VMEM((rows, 2 * half), jnp.float32),
            pltpu.SemaphoreType.DMA((3 + len(ends),)),
        ],
        compiler_params=pltpu.CompilerParams(vmem_limit_bytes=32 * MIB),
        cost_estimate=pl.CostEstimate(
            flops=8 * freqs * blocks * modes * points,
            transcendentals=0,
            bytes_accessed=2 * (spectra.size + eigvecs.size),
        ),
        name="project",
    )(*(pltpu.with_memory_space_constraint(operand, pltpu.HBM) for operand in operands))


def gather_terms(chip, arrived, beside, factor, copies):
    def kernel(chip_ref, arrived_ref, beside_ref, out_ref):
        value = (chip_ref[...] + arrived_ref[...] + beside_ref[...]) * factor
        for copy in range(copies):
            out_ref[copy] = value

    return pl.pallas_call(
        kernel,
        out_shape=jax.ShapeDtypeStruct((copies, *chip.shape), chip.dtype),
        in_specs=[pl.BlockSpec(memory_space=pltpu.VMEM)] * 3,
        out_specs=pl.BlockSpec(memory_space=pltpu.VMEM),
        compiler_params=pltpu.CompilerParams(vmem_limit_bytes=4 * MIB),
        cost_estimate=pl.CostEstimate(
            flops=3 * chip.size, transcendentals=0, bytes_accessed=4 * copies * chip.size
        ),
        name="gather_terms",
    )(chip, arrived, beside)


def sum_over_space(partial, factor, copies):
    count = lax.axis_size("space")
    chips = count // 2

    def beside(value):
        return lax.ppermute(value, "space", [(i, i ^ 1) for i in range(count)])

    def around(value, hops):
        pairs = [(2 * z, 2 * ((z + hops) % chips)) for z in range(chips)]
        if 2 * hops != chips:
            pairs += [(2 * z + 1, 2 * ((z - hops) % chips) + 1) for z in range(chips)]
        return lax.ppermute(value, "space", pairs)

    chip = partial + beside(partial)
    arrived = sum(around(chip, hops) for hops in range(1, chips // 2 + 1))
    return gather_terms(chip, arrived, beside(arrived), factor, copies)


def transform_table(length, groups):
    sample = np.arange(length)
    phase = 2.0 * np.pi * ((sample[:, None] * sample[None, :]) % length) / length
    window = np.sin(np.pi * (sample + 0.5) / length) / math.sqrt(length)
    table = np.stack([np.cos(phase), -np.sin(phase)], axis=1) * window[:, None, None]
    table = table.reshape(length, 2, groups, length // groups).transpose(0, 2, 1, 3)
    return jnp.asarray(table.reshape(length, 2 * length), jnp.bfloat16)


def synthesize(coefficients, moved_modes, table):
    groups, blocks, lanes = coefficients.shape
    columns = moved_modes.shape[2]
    length = table.shape[0]
    freqs = length // groups
    modes = lanes // (2 * freqs)
    half_lanes = lanes // 2
    half = length // 2

    def kernel(coef_ref, modes_ref, table_ref, out_ref, high, low, rebuilt, result, done):
        lane = lax.broadcasted_iota(jnp.int32, (freqs, lanes), 1)
        row = lax.broadcasted_iota(jnp.int32, (freqs, lanes), 0)
        own = jnp.where((lane % half_lanes) // modes == row, 1.0, 0.0)
        signed = jnp.where(lane < half_lanes, own, -own)
        for group in range(groups):
            plain = coef_ref[group]
            for kind, value in enumerate((plain, pltpu.roll(plain, half_lanes, 1))):
                rounded = value.astype(jnp.bfloat16).astype(jnp.float32)
                high[kind, group] = rounded
                low[kind, group] = value - rounded
        for group in range(groups):
            tiles = []
            for block in range(blocks):
                for kind, mask in enumerate((signed, own)):
                    tiles.append(
                        jnp.concatenate(
                            [
                                (jnp.broadcast_to(
                                    side[kind, group, pl.ds(block, 1), :], (freqs, lanes)
                                ) * mask).astype(jnp.bfloat16)
                                for side in (high, low)
                            ],
                            axis=1,
                        )
                    )
            values = modes_ref[group]
            product = jnp.dot(
                jnp.concatenate(tiles, axis=0),
                jnp.concatenate([values, values], axis=0),
                preferred_element_type=jnp.float32,
            )
            rebuilt[:, group * 2 * freqs : (group + 1) * 2 * freqs, :] = product.astype(
                jnp.bfloat16
            ).reshape(blocks, 2 * freqs, columns)
        result[0] = jnp.zeros((half, columns), jnp.float32)

        def send(block):
            return pltpu.make_async_copy(result.at[block], out_ref.at[block], done.at[block])

        for block in range(blocks):
            series = jnp.dot(table_ref[...], rebuilt[block], preferred_element_type=jnp.float32)
            result[block] += series[:half]
            result[block + 1] = series[half:]
            send(block).start()
        send(blocks).start()
        for block in range(blocks + 1):
            send(block).wait()

    return pl.pallas_call(
        kernel,
        out_shape=jax.ShapeDtypeStruct((blocks + 1, half, columns), jnp.float32),
        in_specs=[pl.BlockSpec(memory_space=pltpu.VMEM)] * 3,
        out_specs=pl.BlockSpec(memory_space=pl.ANY),
        scratch_shapes=[
            pltpu.VMEM((2, groups, blocks, lanes), jnp.float32),
            pltpu.VMEM((2, groups, blocks, lanes), jnp.float32),
            pltpu.VMEM((blocks, 2 * length, columns), jnp.bfloat16),
            pltpu.VMEM((blocks + 1, half, columns), jnp.float32),
            pltpu.SemaphoreType.DMA((blocks + 1,)),
        ],
        compiler_params=pltpu.CompilerParams(vmem_limit_bytes=32 * MIB),
        cost_estimate=pl.CostEstimate(
            flops=4 * length * length * blocks * columns,
            transcendentals=0,
            bytes_accessed=4 * (blocks + 1) * half * columns,
        ),
        name="synthesize",
    )(coefficients, moved_modes, table)


def body(spectra, eigvecs, weights):
    _, freqs, _, points_dev = spectra.shape
    groups = lax.axis_size("freq")
    factor = 1.0 / math.sqrt(points_dev * lax.axis_size("space"))
    partial, pieces = project(spectra, eigvecs, weights, groups)
    moved = lax.all_to_all(pieces, "freq", split_axis=0, concat_axis=0, tiled=True)
    copies = sum_over_space(partial, factor, groups)
    copies, moved = lax.optimization_barrier((copies, moved))
    gathered = lax.all_to_all(copies, "freq", split_axis=0, concat_axis=0, tiled=True)
    filtered = synthesize(
        gathered,
        moved.reshape(groups, -1, moved.shape[-1]),
        transform_table(groups * freqs, groups),
    )
    return filtered.reshape(-1, filtered.shape[-1])


def solution(mesh):
    placed = (P(None, "freq", None, "space"), P(None, "freq", None, "space"), P("space"))
    return jax.shard_map(
        body, mesh=mesh, in_specs=placed, out_specs=P(None, ("space", "freq")), check_vma=False
    )
```

time: 56.2 us -> 52 us (0.925)
  blocking collectives: 25.5 us -> 0 us
  starting transfers between devices: 10 us -> 29.8 us
  waiting for transfers between devices: 8.44 us -> 11.4 us
  Pallas kernels: 11.9 us -> 10.1 us
    all_to_all x1 -> x0, blocking collectives: 25.5 us -> none  [body(): lax.all_to_all(pieces, 'freq', split_axis=0, concat_axis=0, tiled=True)]
    ppermute x0 -> x6, starting transfers between devices: none -> 15.4 us  [the longest x4 7.93 us: around(): return lax.ppermute(value, 'space', pairs)]
    ppermute x0 -> x6, waiting for transfers between devices: none -> 4.67 us  [the longest x4 3 us: around(): return lax.ppermute(value, 'space', pairs)]
    all_to_all x1 -> x2, starting transfers between devices: 10 us -> 14.5 us  [the longest x1 7.6 us: body(): lax.all_to_all(pieces, 'freq', split_axis=0, concat_axis=0, tiled=True)]
    pallas_call x3 -> x2, Pallas kernels: 7.38 us -> 5.62 us  [the longest x1 4.92 us: project(): pl.pallas_call(kernel, out_shape=[jax.ShapeDtypeStruct((blocks, 2 * half)...]
    all_to_all x1 -> x2, waiting for transfers between devices: 8.44 us -> 6.74 us  [the longest x1 6.73 us: body(): lax.all_to_all(copies, 'freq', split_axis=0, concat_axis=0, tiled=True)]
  transfers between devices with their start and end apart: 1 -> 8, of which waited for: 1 -> 5; matrix products, arithmetic and copies ran while one was open for 0% -> 1% of each run, Pallas kernels for 3% -> 1%
where the time goes in v2:
time: 52 us; the launch traced here: 51.7 us
  starting transfers between devices  29.8 us (57%)
  waiting for transfers between devices  11.4 us (22%)
  Pallas kernels  10.1 us (19%)
    ppermute x4, starting transfers between devices, around(): return lax.ppermute(value, 'space', pairs)  7.93 us
    all_to_all x1, starting transfers between devices, body(): lax.all_to_all(pieces, 'freq', split_axis=0, concat_axis=0, tiled=True)  7.6 us
    ppermute x2, starting transfers between devices, beside(): return lax.ppermute(value, 'space', [(i, i ^ 1) for i in range(count)])  7.44 us
    all_to_all x1, starting transfers between devices, body(): lax.all_to_all(copies, 'freq', split_axis=0, concat_axis=0, tiled=True)  6.85 us
    all_to_all x1, waiting for transfers between devices, body(): lax.all_to_all(copies, 'freq', split_axis=0, concat_axis=0, tiled=True)  6.73 us
    pallas_call x1, Pallas kernels, project(): pl.pallas_call(kernel, out_shape=[jax.ShapeDtypeStruct((blocks, 2 * half)...  4.92 us
    pallas_call x1, Pallas kernels, synthesize(): pl.pallas_call(kernel, out_shape=jax.ShapeDtypeStruct((blocks + 1, half,...  4.51 us
    ppermute x4, waiting for transfers between devices, around(): return lax.ppermute(value, 'space', pairs)  3 us
  transfers between devices with their start and end apart: 8, of which 5 were waited for; matrix products, arithmetic and copies ran while one was open for 1% of the time, Pallas kernels for 1%

profile of v2, /device:TPU:1, one launch (start us, length us, event | category | flops | bytes accessed | tf_op | source)
XLA Modules:
  0.0 51.7 jit_solution(17499783363088586905)
XLA Ops:
  0.0 0.0 copy-start
  0.0 4.9 %project.1 = (f32[24,128]{1,0:T(8,128)S(1)}, bf16[16,2,16,4,256]{4,3,2,1,0:T(4,128)(2,1)}) custom-call(bf16[768,4096]{1,0:T(8,128)(2,1)} %bitcast.3, bf16[2,16,4,4096]{3,2,1,0:T(4,128)(2,1)} %eigvecs_hbm.1, bf16[32,128]{1,0:T(8,128)(2,1)} %bitcast.4), custom_call_target="tpu_custom_call" | custom-call | flops 50331648 | bytes 7340032 | tf_op jit(solution)/shard_map/project/pallas_call | solution.py:76
  4.9 7.6 %all-to-all-start = ((bf16[16,2,16,4,256]{4,3,2,1,0:T(4,128)(2,1)}), bf16[16,2,16,4,256]{4,3,2,1,0:T(4,128)(2,1)S(1)}, u32[]{:S(2)}, u32[]{:S(2)}) async-start(bf16[16,2,16,4,256]{4,3,2,1,0:T(4,128)(2,1)} %get-tuple-element.10), calls=%async_computation | async-start | bytes 2097152 | tf_op jit(solution)/shard_map/all_to_all | solution.py:234
  12.5 1.0 %collective-permute-start = (f32[24,128]{1,0:T(8,128)S(1)}, f32[24,128]{1,0:T(8,128)S(1)}, u32[]{:S(2)}, u32[]{:S(2)}) collective-permute-start(f32[24,128]{1,0:T(8,128)S(1)} %get-tuple-element.9), channel_id=1, source_target_pairs={{0,1},{1,0},{2,3},{3,2},{4,5},{5,4},{6,7},{7,6},{8,9},{9,8},{10,11... | collective-permute-start | bytes 36872 | tf_op jit(solution)/shard_map/ppermute | solution.py:127
  13.6 0.8 %collective-permute-done = f32[24,128]{1,0:T(8,128)S(1)} collective-permute-done((f32[24,128]{1,0:T(8,128)S(1)}, f32[24,128]{1,0:T(8,128)S(1)}, u32[]{:S(2)}, u32[]{:S(2)}) %collective-permute-start) | collective-permute-done | bytes 12320 | tf_op jit(solution)/shard_map/ppermute | solution.py:127
  14.4 0.7 %collective-permute-start.4 = (f32[24,128]{1,0:T(8,128)S(1)}, f32[24,128]{1,0:T(8,128)S(1)}, u32[]{:S(2)}, u32[]{:S(2)}) collective-permute-start(f32[24,128]{1,0:T(8,128)S(1)} %add.12.chip_ref), channel_id=1, source_target_pairs={{0,8},{2,10},{4,12},{6,14},{8,0},{10,2},{12,4},{14,6},{16,24},{18,... | collective-permute-start | bytes 36872 | tf_op jit(solution)/shard_map/ppermute | solution.py:133
  15.1 6.5 %collective-permute-start.3 = (f32[24,128]{1,0:T(8,128)S(1)}, f32[24,128]{1,0:T(8,128)S(1)}, u32[]{:S(2)}, u32[]{:S(2)}) collective-permute-start(f32[24,128]{1,0:T(8,128)S(1)} %add.12.chip_ref), channel_id=1, source_target_pairs={{0,6},{2,8},{4,10},{6,12},{8,14},{10,0},{12,2},{14,4},{1,11},{3,13... | collective-permute-start | bytes 36872 | tf_op jit(solution)/shard_map/ppermute | solution.py:133
  21.6 0.3 collective-permute-start.2
  21.9 0.5 collective-permute-start.1
  22.4 0.0 collective-permute-done.4
  22.4 0.1 collective-permute-done.3
  22.4 2.9 %collective-permute-done.2 = f32[24,128]{1,0:T(8,128)S(1)} collective-permute-done((f32[24,128]{1,0:T(8,128)S(1)}, f32[24,128]{1,0:T(8,128)S(1)}, u32[]{:S(2)}, u32[]{:S(2)}) %collective-permute-start.2) | collective-permute-done | bytes 12320 | tf_op jit(solution)/shard_map/ppermute | solution.py:133
  25.4 0.0 collective-permute-done.1
  25.4 6.4 %collective-permute-start.5 = (f32[24,128]{1,0:T(8,128)S(1)}, f32[24,128]{1,0:T(8,128)S(1)}, u32[]{:S(2)}, u32[]{:S(2)}) collective-permute-start(f32[24,128]{1,0:T(8,128)S(1)} %add_add_fusion.arrived_ref), channel_id=1, source_target_pairs={{0,1},{1,0},{2,3},{3,2},{4,5},{5,4},{6,7},{7,6},{8,9},{9,8},{10,11... | collective-permute-start | bytes 36872 | tf_op jit(solution)/shard_map/ppermute | solution.py:127
  31.8 0.8 %collective-permute-done.5.beside_ref = f32[24,128]{1,0:T(8,128)S(1)} collective-permute-done((f32[24,128]{1,0:T(8,128)S(1)}, f32[24,128]{1,0:T(8,128)S(1)}, u32[]{:S(2)}, u32[]{:S(2)}) %collective-permute-start.5) | collective-permute-done | bytes 12320 | tf_op jit(solution)/shard_map/ppermute | solution.py:127
  32.6 0.7 %gather_terms.1 = f32[16,24,128]{2,1,0:T(8,128)} custom-call(f32[24,128]{1,0:T(8,128)S(1)} %add.12.chip_ref, f32[24,128]{1,0:T(8,128)S(1)} %add_add_fusion.arrived_ref, f32[24,128]{1,0:T(8,128)S(1)} %collective-permute-done.5.beside_ref), custom_call_target="tpu_custom_call" | custom-call | flops 9216 | bytes 196608 | tf_op jit(solution)/shard_map/gather_terms/pallas_call | solution.py:109
  33.3 0.0 all-to-all-done
  33.3 6.9 %all-to-all-start.1 = ((f32[16,24,128]{2,1,0:T(8,128)}), f32[16,24,128]{2,1,0:T(8,128)S(1)}, u32[]{:S(2)}, u32[]{:S(2)}) async-start(f32[16,24,128]{2,1,0:T(8,128)} %gather_terms.1), calls=%async_computation.1 | async-start | bytes 393216 | tf_op jit(solution)/shard_map/all_to_all | solution.py:237
  40.2 0.3 reshape.14.modes_ref
  40.5 6.7 %all-to-all-done.1.coef_ref = f32[16,24,128]{2,1,0:T(8,128)S(1)} async-done(((f32[16,24,128]{2,1,0:T(8,128)}), f32[16,24,128]{2,1,0:T(8,128)S(1)}, u32[]{:S(2)}, u32[]{:S(2)}) %all-to-all-start.1) | async-done | bytes 196640 | tf_op jit(solution)/shard_map/all_to_all | solution.py:237
  47.2 0.0 copy-done
  47.2 4.5 %synthesize.1 = f32[25,128,256]{2,1,0:T(8,128)} custom-call(f32[16,24,128]{2,1,0:T(8,128)S(1)} %all-to-all-done.1.coef_ref, bf16[16,128,256]{2,1,0:T(8,128)(2,1)S(1)} %reshape.14.modes_ref, bf16[256,512]{1,0:T(8,128)(2,1)S(1)} %copy-done), custom_call_target="tpu_custom_call" | custom-call | flops 1610612736 | bytes 3276800 | tf_op jit(solution)/shard_map/synthesize/pallas_call | solution.py:207
  (2 shorter events, 0.0 us)
Async XLA Ops:
  0.0 47.2 %copy-start = (bf16[256,512]{1,0:T(8,128)(2,1)S(1)}, bf16[256,512]{1,0:T(8,128)(2,1)}, u32[]{:S(2)}) copy-start(bf16[256,512]{1,0:T(8,128)(2,1)} %constant.2.clone.table_ref) | copy-start | bytes 786436
  4.9 28.4 %all-to-all-start = ((bf16[16,2,16,4,256]{4,3,2,1,0:T(4,128)(2,1)}), bf16[16,2,16,4,256]{4,3,2,1,0:T(4,128)(2,1)S(1)}, u32[]{:S(2)}, u32[]{:S(2)}) async-start(bf16[16,2,16,4,256]{4,3,2,1,0:T(4,128)(2,1)} %get-tuple-element.10), calls=%async_computation | async-start | bytes 2097152 | tf_op jit(solution)/shard_map/all_to_all | solution.py:234
  12.5 1.9 %collective-permute-start = (f32[24,128]{1,0:T(8,128)S(1)}, f32[24,128]{1,0:T(8,128)S(1)}, u32[]{:S(2)}, u32[]{:S(2)}) collective-permute-start(f32[24,128]{1,0:T(8,128)S(1)} %get-tuple-element.9), channel_id=1, source_target_pairs={{0,1},{1,0},{2,3},{3,2},{4,5},{5,4},{6,7},{7,6},{8,9},{9,8},{10,11... | collective-permute-start | bytes 36872 | tf_op jit(solution)/shard_map/ppermute | solution.py:127
  14.4 7.9 %collective-permute-start.4 = (f32[24,128]{1,0:T(8,128)S(1)}, f32[24,128]{1,0:T(8,128)S(1)}, u32[]{:S(2)}, u32[]{:S(2)}) collective-permute-start(f32[24,128]{1,0:T(8,128)S(1)} %add.12.chip_ref), channel_id=1, source_target_pairs={{0,8},{2,10},{4,12},{6,14},{8,0},{10,2},{12,4},{14,6},{16,24},{18,... | collective-permute-start | bytes 36872 | tf_op jit(solution)/shard_map/ppermute | solution.py:133
  15.1 7.4 %collective-permute-start.3 = (f32[24,128]{1,0:T(8,128)S(1)}, f32[24,128]{1,0:T(8,128)S(1)}, u32[]{:S(2)}, u32[]{:S(2)}) collective-permute-start(f32[24,128]{1,0:T(8,128)S(1)} %add.12.chip_ref), channel_id=1, source_target_pairs={{0,6},{2,8},{4,10},{6,12},{8,14},{10,0},{12,2},{14,4},{1,11},{3,13... | collective-permute-start | bytes 36872 | tf_op jit(solution)/shard_map/ppermute | solution.py:133
  21.6 3.7 %collective-permute-start.2 = (f32[24,128]{1,0:T(8,128)S(1)}, f32[24,128]{1,0:T(8,128)S(1)}, u32[]{:S(2)}, u32[]{:S(2)}) collective-permute-start(f32[24,128]{1,0:T(8,128)S(1)} %add.12.chip_ref), channel_id=1, source_target_pairs={{0,4},{2,6},{4,8},{6,10},{8,12},{10,14},{12,0},{14,2},{1,13},{3,15... | collective-permute-start | bytes 36872 | tf_op jit(solution)/shard_map/ppermute | solution.py:133
  21.9 3.5 %collective-permute-start.1 = (f32[24,128]{1,0:T(8,128)S(1)}, f32[24,128]{1,0:T(8,128)S(1)}, u32[]{:S(2)}, u32[]{:S(2)}) collective-permute-start(f32[24,128]{1,0:T(8,128)S(1)} %add.12.chip_ref), channel_id=1, source_target_pairs={{0,2},{2,4},{4,6},{6,8},{8,10},{10,12},{12,14},{14,0},{1,15},{3,1}... | collective-permute-start | bytes 36872 | tf_op jit(solution)/shard_map/ppermute | solution.py:133
  25.4 7.2 %collective-permute-start.5 = (f32[24,128]{1,0:T(8,128)S(1)}, f32[24,128]{1,0:T(8,128)S(1)}, u32[]{:S(2)}, u32[]{:S(2)}) collective-permute-start(f32[24,128]{1,0:T(8,128)S(1)} %add_add_fusion.arrived_ref), channel_id=1, source_target_pairs={{0,1},{1,0},{2,3},{3,2},{4,5},{5,4},{6,7},{7,6},{8,9},{9,8},{10,11... | collective-permute-start | bytes 36872 | tf_op jit(solution)/shard_map/ppermute | solution.py:127
  33.3 13.9 %all-to-all-start.1 = ((f32[16,24,128]{2,1,0:T(8,128)}), f32[16,24,128]{2,1,0:T(8,128)S(1)}, u32[]{:S(2)}, u32[]{:S(2)}) async-start(f32[16,24,128]{2,1,0:T(8,128)} %gather_terms.1), calls=%async_computation.1 | async-start | bytes 393216 | tf_op jit(solution)/shard_map/all_to_all | solution.py:237

commit v3 on v2

--- a/solution.py
+++ b/solution.py
@@ -10,6 +10,8 @@
 
 MIB = 1024 * 1024
 LANES = 128
+SLAB = 4
+HOPS_BY_CORE = ((0, -2), (-1, 2), (1, 3), (4, -3))
 
 
 def project(spectra, eigvecs, weights, parts):
@@ -23,8 +25,8 @@
     dtype = spectra.dtype
 
     def kernel(
-        spectra_hbm, eigvecs_hbm, weights_hbm, out_ref, pieces_ref,
-        spectra_ref, eigvecs_ref, weights_ref, weighted, columns, total, done,
+        spectra_hbm, eigvecs_hbm, weights_hbm, out_ref, pieces_hbm,
+        spectra_ref, eigvecs_ref, weights_ref, weighted, columns, total, pieces_ref, done, sent,
     ):
         small = pltpu.make_async_copy(weights_hbm, weights_ref, done.at[0])
         small.start()
@@ -52,8 +54,17 @@
                     eigvecs_ref[part, k].astype(jnp.float32) * scale
                 )
         columns[...] = jnp.transpose(weighted[...]).astype(dtype)
+        slabs = []
         for piece in range(parts):
             pieces_ref[piece] = eigvecs_ref[:, :, :, piece * width : (piece + 1) * width]
+            if piece % SLAB == SLAB - 1:
+                some = pl.ds(piece + 1 - SLAB, SLAB)
+                slabs.append(
+                    pltpu.make_async_copy(
+                        pieces_ref.at[some], pieces_hbm.at[some], sent.at[len(slabs)]
+                    )
+                )
+                slabs[-1].start()
         for copy, start, end in zip(by_rows, starts, ends):
             copy.wait()
             total[start:end] = jnp.dot(
@@ -69,6 +80,8 @@
                 kept = jnp.where(own, total[first : first + blocks], kept)
             sums.append(kept)
         out_ref[...] = jnp.where(lane < half, sums[0], -sums[0]) + pltpu.roll(sums[1], half, 1)
+        for copy in slabs:
+            copy.wait()
 
     operands = (
         spectra.reshape(rows, points), eigvecs, weights.reshape(points // LANES, LANES)
@@ -80,7 +93,7 @@
             jax.ShapeDtypeStruct((parts, 2, freqs, modes, width), dtype),
         ],
         in_specs=[pl.BlockSpec(memory_space=pl.ANY)] * 3,
-        out_specs=[pl.BlockSpec(memory_space=pltpu.VMEM)] * 2,
+        out_specs=[pl.BlockSpec(memory_space=pltpu.VMEM), pl.BlockSpec(memory_space=pl.ANY)],
         scratch_shapes=[
             pltpu.VMEM((rows, points), dtype),
             pltpu.VMEM(eigvecs.shape, dtype),
@@ -88,7 +101,9 @@
             pltpu.VMEM((2 * half, points), jnp.float32),
             pltpu.VMEM((points, 2 * half), dtype),
             pltpu.VMEM((rows, 2 * half), jnp.float32),
+            pltpu.VMEM((parts, 2, freqs, modes, width), dtype),
             pltpu.SemaphoreType.DMA((3 + len(ends),)),
+            pltpu.SemaphoreType.DMA((parts // SLAB,)),
         ],
         compiler_params=pltpu.CompilerParams(vmem_limit_bytes=32 * MIB),
         cost_estimate=pl.CostEstimate(
@@ -108,7 +123,7 @@
 
     return pl.pallas_call(
         kernel,
-        out_shape=jax.ShapeDtypeStruct((copies, *chip.shape), chip.dtype),
+        out_shape=pltpu.VMEM((copies, *chip.shape), chip.dtype),
         in_specs=[pl.BlockSpec(memory_space=pltpu.VMEM)] * 3,
         out_specs=pl.BlockSpec(memory_space=pltpu.VMEM),
         compiler_params=pltpu.CompilerParams(vmem_limit_bytes=4 * MIB),
@@ -126,14 +141,17 @@
     def beside(value):
         return lax.ppermute(value, "space", [(i, i ^ 1) for i in range(count)])
 
-    def around(value, hops):
-        pairs = [(2 * z, 2 * ((z + hops) % chips)) for z in range(chips)]
-        if 2 * hops != chips:
-            pairs += [(2 * z + 1, 2 * ((z - hops) % chips) + 1) for z in range(chips)]
+    def around(value, by_core):
+        pairs = []
+        for core, hops in enumerate(by_core):
+            if hops:
+                pairs += [
+                    (2 * z + core, 2 * ((z + hops) % chips) + core) for z in range(chips)
+                ]
         return lax.ppermute(value, "space", pairs)
 
     chip = partial + beside(partial)
-    arrived = sum(around(chip, hops) for hops in range(1, chips // 2 + 1))
+    arrived = sum(around(chip, by_core) for by_core in HOPS_BY_CORE)
     return gather_terms(chip, arrived, beside(arrived), factor, copies)
 
 

time: 52 us -> 49.2 us (0.946)
  the two profiles are of different devices: /device:TPU:1 before, /device:TPU:96 now
where the time goes in v3:
time: 49.2 us; the launch traced here: 48.9 us
  starting transfers between devices  26.4 us (54%)
  waiting for transfers between devices  12.4 us (25%)
  Pallas kernels  9.78 us (20%)
    all_to_all x1, waiting for transfers between devices, body(): lax.all_to_all(copies, 'freq', split_axis=0, concat_axis=0, tiled=True)  8.06 us
    ppermute x4, starting transfers between devices, around(): return lax.ppermute(value, 'space', pairs)  7.17 us
    all_to_all x1, starting transfers between devices, body(): lax.all_to_all(pieces, 'freq', split_axis=0, concat_axis=0, tiled=True)  7.05 us
    all_to_all x1, starting transfers between devices, body(): lax.all_to_all(copies, 'freq', split_axis=0, concat_axis=0, tiled=True)  6.72 us
    ppermute x2, starting transfers between devices, beside(): return lax.ppermute(value, 'space', [(i, i ^ 1) for i in range(count)])  5.46 us
    pallas_call x1, Pallas kernels, project(): pl.pallas_call(kernel, out_shape=[jax.ShapeDtypeStruct((blocks, 2 * half)...  4.58 us
    pallas_call x1, Pallas kernels, synthesize(): pl.pallas_call(kernel, out_shape=jax.ShapeDtypeStruct((blocks + 1, half,...  4.51 us
    ppermute x4, waiting for transfers between devices, around(): return lax.ppermute(value, 'space', pairs)  2.23 us
  transfers between devices with their start and end apart: 8, of which 7 were waited for; matrix products, arithmetic and copies ran while one was open for 1% of the time, Pallas kernels for 1%

profile of v3, /device:TPU:96, one launch (start us, length us, event | category | flops | bytes accessed | tf_op | source)
XLA Modules:
  0.0 48.9 jit_solution(80678923140808546)
XLA Ops:
  0.0 0.0 copy-start
  0.0 4.6 %project.1 = (f32[24,128]{1,0:T(8,128)S(1)}, bf16[16,2,16,4,256]{4,3,2,1,0:T(4,128)(2,1)}) custom-call(bf16[768,4096]{1,0:T(8,128)(2,1)} %bitcast.3, bf16[2,16,4,4096]{3,2,1,0:T(4,128)(2,1)} %eigvecs_hbm.1, bf16[32,128]{1,0:T(8,128)(2,1)} %bitcast.4), custom_call_target="tpu_custom_call" | custom-call | flops 50331648 | bytes 7340032 | tf_op jit(solution)/shard_map/project/pallas_call | solution.py:89
  4.6 7.0 %all-to-all-start = ((bf16[16,2,16,4,256]{4,3,2,1,0:T(4,128)(2,1)}), bf16[16,2,16,4,256]{4,3,2,1,0:T(4,128)(2,1)S(1)}, u32[]{:S(2)}, u32[]{:S(2)}) async-start(bf16[16,2,16,4,256]{4,3,2,1,0:T(4,128)(2,1)} %get-tuple-element.10), calls=%async_computation | async-start | bytes 2097152 | tf_op jit(solution)/shard_map/all_to_all | solution.py:252
  11.6 0.1 collective-permute-start
  11.7 1.2 %collective-permute-done = f32[24,128]{1,0:T(8,128)S(1)} collective-permute-done((f32[24,128]{1,0:T(8,128)S(1)}, f32[24,128]{1,0:T(8,128)S(1)}, u32[]{:S(2)}, u32[]{:S(2)}) %collective-permute-start) | collective-permute-done | bytes 12320 | tf_op jit(solution)/shard_map/ppermute | solution.py:142
  12.9 4.5 %collective-permute-start.4 = (f32[24,128]{1,0:T(8,128)S(1)}, f32[24,128]{1,0:T(8,128)S(1)}, u32[]{:S(2)}, u32[]{:S(2)}) collective-permute-start(f32[24,128]{1,0:T(8,128)S(1)} %add.12.chip_ref), channel_id=1, source_target_pairs={{0,8},{2,10},{4,12},{6,14},{8,0},{10,2},{12,4},{14,6},{1,11},{3,13... | collective-permute-start | bytes 36872 | tf_op jit(solution)/shard_map/ppermute | solution.py:151
  17.4 0.0 collective-permute-start.3
  17.4 2.0 %collective-permute-start.2 = (f32[24,128]{1,0:T(8,128)S(1)}, f32[24,128]{1,0:T(8,128)S(1)}, u32[]{:S(2)}, u32[]{:S(2)}) collective-permute-start(f32[24,128]{1,0:T(8,128)S(1)} %add.12.chip_ref), channel_id=1, source_target_pairs={{0,14},{2,0},{4,2},{6,4},{8,6},{10,8},{12,10},{14,12},{1,5},{3,7},... | collective-permute-start | bytes 36872 | tf_op jit(solution)/shard_map/ppermute | solution.py:151
  19.4 0.7 %collective-permute-start.1 = (f32[24,128]{1,0:T(8,128)S(1)}, f32[24,128]{1,0:T(8,128)S(1)}, u32[]{:S(2)}, u32[]{:S(2)}) collective-permute-start(f32[24,128]{1,0:T(8,128)S(1)} %add.12.chip_ref), channel_id=1, source_target_pairs={{1,13},{3,15},{5,1},{7,3},{9,5},{11,7},{13,9},{15,11},{17,29},{19,... | collective-permute-start | bytes 36872 | tf_op jit(solution)/shard_map/ppermute | solution.py:151
  20.1 0.4 collective-permute-done.4
  20.5 0.8 %collective-permute-done.3 = f32[24,128]{1,0:T(8,128)S(1)} collective-permute-done((f32[24,128]{1,0:T(8,128)S(1)}, f32[24,128]{1,0:T(8,128)S(1)}, u32[]{:S(2)}, u32[]{:S(2)}) %collective-permute-start.3) | collective-permute-done | bytes 12320 | tf_op jit(solution)/shard_map/ppermute | solution.py:151
  21.3 1.0 %collective-permute-done.2 = f32[24,128]{1,0:T(8,128)S(1)} collective-permute-done((f32[24,128]{1,0:T(8,128)S(1)}, f32[24,128]{1,0:T(8,128)S(1)}, u32[]{:S(2)}, u32[]{:S(2)}) %collective-permute-start.2) | collective-permute-done | bytes 12320 | tf_op jit(solution)/shard_map/ppermute | solution.py:151
  22.3 0.0 collective-permute-done.1
  22.3 5.4 %collective-permute-start.5 = (f32[24,128]{1,0:T(8,128)S(1)}, f32[24,128]{1,0:T(8,128)S(1)}, u32[]{:S(2)}, u32[]{:S(2)}) collective-permute-start(f32[24,128]{1,0:T(8,128)S(1)} %add_add_fusion.arrived_ref), channel_id=1, source_target_pairs={{0,1},{1,0},{2,3},{3,2},{4,5},{5,4},{6,7},{7,6},{8,9},{9,8},{10,11... | collective-permute-start | bytes 36872 | tf_op jit(solution)/shard_map/ppermute | solution.py:142
  27.7 0.8 %collective-permute-done.5.beside_ref = f32[24,128]{1,0:T(8,128)S(1)} collective-permute-done((f32[24,128]{1,0:T(8,128)S(1)}, f32[24,128]{1,0:T(8,128)S(1)}, u32[]{:S(2)}, u32[]{:S(2)}) %collective-permute-start.5) | collective-permute-done | bytes 12320 | tf_op jit(solution)/shard_map/ppermute | solution.py:142
  28.5 0.7 %gather_terms.1 = f32[16,24,128]{2,1,0:T(8,128)} custom-call(f32[24,128]{1,0:T(8,128)S(1)} %add.12.chip_ref, f32[24,128]{1,0:T(8,128)S(1)} %add_add_fusion.arrived_ref, f32[24,128]{1,0:T(8,128)S(1)} %collective-permute-done.5.beside_ref), custom_call_target="tpu_custom_call" | custom-call | flops 9216 | bytes 196608 | tf_op jit(solution)/shard_map/gather_terms/pallas_call | solution.py:124
  29.2 0.1 all-to-all-done
  29.3 6.7 %all-to-all-start.1 = ((f32[16,24,128]{2,1,0:T(8,128)}), f32[16,24,128]{2,1,0:T(8,128)S(1)}, u32[]{:S(2)}, u32[]{:S(2)}) async-start(f32[16,24,128]{2,1,0:T(8,128)} %gather_terms.1), calls=%async_computation.1 | async-start | bytes 393216 | tf_op jit(solution)/shard_map/all_to_all | solution.py:255
  36.1 0.3 reshape.14.modes_ref
  36.4 8.1 %all-to-all-done.1.coef_ref = f32[16,24,128]{2,1,0:T(8,128)S(1)} async-done(((f32[16,24,128]{2,1,0:T(8,128)}), f32[16,24,128]{2,1,0:T(8,128)S(1)}, u32[]{:S(2)}, u32[]{:S(2)}) %all-to-all-start.1) | async-done | bytes 196640 | tf_op jit(solution)/shard_map/all_to_all | solution.py:255
  44.4 0.0 copy-done
  44.4 4.5 %synthesize.1 = f32[25,128,256]{2,1,0:T(8,128)} custom-call(f32[16,24,128]{2,1,0:T(8,128)S(1)} %all-to-all-done.1.coef_ref, bf16[16,128,256]{2,1,0:T(8,128)(2,1)S(1)} %reshape.14.modes_ref, bf16[256,512]{1,0:T(8,128)(2,1)S(1)} %copy-done), custom_call_target="tpu_custom_call" | custom-call | flops 1610612736 | bytes 3276800 | tf_op jit(solution)/shard_map/synthesize/pallas_call | solution.py:225
  (2 shorter events, 0.0 us)
Async XLA Ops:
  0.0 44.4 %copy-start = (bf16[256,512]{1,0:T(8,128)(2,1)S(1)}, bf16[256,512]{1,0:T(8,128)(2,1)}, u32[]{:S(2)}) copy-start(bf16[256,512]{1,0:T(8,128)(2,1)} %constant.2.clone.table_ref) | copy-start | bytes 786436
  4.6 24.8 %all-to-all-start = ((bf16[16,2,16,4,256]{4,3,2,1,0:T(4,128)(2,1)}), bf16[16,2,16,4,256]{4,3,2,1,0:T(4,128)(2,1)S(1)}, u32[]{:S(2)}, u32[]{:S(2)}) async-start(bf16[16,2,16,4,256]{4,3,2,1,0:T(4,128)(2,1)} %get-tuple-element.10), calls=%async_computation | async-start | bytes 2097152 | tf_op jit(solution)/shard_map/all_to_all | solution.py:252
  11.6 1.3 %collective-permute-start = (f32[24,128]{1,0:T(8,128)S(1)}, f32[24,128]{1,0:T(8,128)S(1)}, u32[]{:S(2)}, u32[]{:S(2)}) collective-permute-start(f32[24,128]{1,0:T(8,128)S(1)} %get-tuple-element.9), channel_id=1, source_target_pairs={{0,1},{1,0},{2,3},{3,2},{4,5},{5,4},{6,7},{7,6},{8,9},{9,8},{10,11... | collective-permute-start | bytes 36872 | tf_op jit(solution)/shard_map/ppermute | solution.py:142
  12.9 7.6 %collective-permute-start.4 = (f32[24,128]{1,0:T(8,128)S(1)}, f32[24,128]{1,0:T(8,128)S(1)}, u32[]{:S(2)}, u32[]{:S(2)}) collective-permute-start(f32[24,128]{1,0:T(8,128)S(1)} %add.12.chip_ref), channel_id=1, source_target_pairs={{0,8},{2,10},{4,12},{6,14},{8,0},{10,2},{12,4},{14,6},{1,11},{3,13... | collective-permute-start | bytes 36872 | tf_op jit(solution)/shard_map/ppermute | solution.py:151
  17.4 3.9 %collective-permute-start.3 = (f32[24,128]{1,0:T(8,128)S(1)}, f32[24,128]{1,0:T(8,128)S(1)}, u32[]{:S(2)}, u32[]{:S(2)}) collective-permute-start(f32[24,128]{1,0:T(8,128)S(1)} %add.12.chip_ref), channel_id=1, source_target_pairs={{0,2},{2,4},{4,6},{6,8},{8,10},{10,12},{12,14},{14,0},{1,7},{3,9},... | collective-permute-start | bytes 36872 | tf_op jit(solution)/shard_map/ppermute | solution.py:151
  17.4 4.9 %collective-permute-start.2 = (f32[24,128]{1,0:T(8,128)S(1)}, f32[24,128]{1,0:T(8,128)S(1)}, u32[]{:S(2)}, u32[]{:S(2)}) collective-permute-start(f32[24,128]{1,0:T(8,128)S(1)} %add.12.chip_ref), channel_id=1, source_target_pairs={{0,14},{2,0},{4,2},{6,4},{8,6},{10,8},{12,10},{14,12},{1,5},{3,7},... | collective-permute-start | bytes 36872 | tf_op jit(solution)/shard_map/ppermute | solution.py:151
  19.4 2.9 %collective-permute-start.1 = (f32[24,128]{1,0:T(8,128)S(1)}, f32[24,128]{1,0:T(8,128)S(1)}, u32[]{:S(2)}, u32[]{:S(2)}) collective-permute-start(f32[24,128]{1,0:T(8,128)S(1)} %add.12.chip_ref), channel_id=1, source_target_pairs={{1,13},{3,15},{5,1},{7,3},{9,5},{11,7},{13,9},{15,11},{17,29},{19,... | collective-permute-start | bytes 36872 | tf_op jit(solution)/shard_map/ppermute | solution.py:151
  22.3 6.2 %collective-permute-start.5 = (f32[24,128]{1,0:T(8,128)S(1)}, f32[24,128]{1,0:T(8,128)S(1)}, u32[]{:S(2)}, u32[]{:S(2)}) collective-permute-start(f32[24,128]{1,0:T(8,128)S(1)} %add_add_fusion.arrived_ref), channel_id=1, source_target_pairs={{0,1},{1,0},{2,3},{3,2},{4,5},{5,4},{6,7},{7,6},{8,9},{9,8},{10,11... | collective-permute-start | bytes 36872 | tf_op jit(solution)/shard_map/ppermute | solution.py:142
  29.3 15.1 %all-to-all-start.1 = ((f32[16,24,128]{2,1,0:T(8,128)}), f32[16,24,128]{2,1,0:T(8,128)S(1)}, u32[]{:S(2)}, u32[]{:S(2)}) async-start(f32[16,24,128]{2,1,0:T(8,128)} %gather_terms.1), calls=%async_computation.1 | async-start | bytes 393216 | tf_op jit(solution)/shard_map/all_to_all | solution.py:255

commit v4 on v3

--- a/solution.py
+++ b/solution.py
@@ -20,7 +20,7 @@
     half = freqs * modes
     rows = 2 * freqs * blocks
     width = points // parts
-    ends = [rows // 4, rows // 2, rows * 3 // 4, rows * 7 // 8, rows]
+    ends = [rows * (i + 1) // 4 for i in range(4)]
     starts = [0, *ends[:-1]]
     dtype = spectra.dtype
 
@@ -155,48 +155,71 @@
     return gather_terms(chip, arrived, beside(arrived), factor, copies)
 
 
-def transform_table(length, groups):
-    sample = np.arange(length)
-    phase = 2.0 * np.pi * ((sample[:, None] * sample[None, :]) % length) / length
-    window = np.sin(np.pi * (sample + 0.5) / length) / math.sqrt(length)
-    table = np.stack([np.cos(phase), -np.sin(phase)], axis=1) * window[:, None, None]
-    table = table.reshape(length, 2, groups, length // groups).transpose(0, 2, 1, 3)
-    return jnp.asarray(table.reshape(length, 2 * length), jnp.bfloat16)
-
-
-def synthesize(coefficients, moved_modes, table):
+def transform_tables(length, groups):
+    freqs = length // groups
+    sample = np.arange(length // 2)
+    phase = 2.0 * np.pi * ((sample[:, None] * np.arange(length)[None, :]) % length) / length
+    table = np.stack([np.cos(phase), -np.sin(phase)], axis=1) / math.sqrt(length)
+    table = table.reshape(length // 2, 2, groups, freqs // 2, 2).transpose(4, 0, 2, 1, 3)
+    window = np.sin(np.pi * (np.arange(length) + 0.5) / length).reshape(2, length // 2, 1)
+    return (
+        jnp.asarray(table.reshape(2, length // 2, length), jnp.bfloat16),
+        jnp.asarray(np.broadcast_to(window, (2, length // 2, LANES)), jnp.float32),
+    )
+
+
+def synthesize(coefficients, moved_modes, table, window):
     groups, blocks, lanes = coefficients.shape
     columns = moved_modes.shape[2]
-    length = table.shape[0]
+    length = table.shape[2]
     freqs = length // groups
     modes = lanes // (2 * freqs)
     half_lanes = lanes // 2
     half = length // 2
-
-    def kernel(coef_ref, modes_ref, table_ref, out_ref, high, low, rebuilt, result, done):
+    pair = freqs // 2
+
+    def kernel(
+        coef_ref, modes_ref, table_ref, window_ref, out_ref, high, low, rebuilt, result, done
+    ):
         lane = lax.broadcasted_iota(jnp.int32, (freqs, lanes), 1)
         row = lax.broadcasted_iota(jnp.int32, (freqs, lanes), 0)
-        own = jnp.where((lane % half_lanes) // modes == row, 1.0, 0.0)
-        signed = jnp.where(lane < half_lanes, own, -own)
+        sign = jnp.where((row < pair) & (lane >= half_lanes), -1.0, 1.0)
+        masks = [
+            jnp.where((lane % half_lanes) // modes == 2 * (row % pair) + odd, sign, 0.0)
+            for odd in range(2)
+        ]
         for group in range(groups):
             plain = coef_ref[group]
             for kind, value in enumerate((plain, pltpu.roll(plain, half_lanes, 1))):
                 rounded = value.astype(jnp.bfloat16).astype(jnp.float32)
                 high[kind, group] = rounded
                 low[kind, group] = value - rounded
+        first = jnp.concatenate([window_ref[0]] * (columns // LANES), axis=1)
+        second = jnp.concatenate([window_ref[1]] * (columns // LANES), axis=1)
+        result[0] = jnp.zeros((half, columns), jnp.float32)
+
+        def send(block):
+            return pltpu.make_async_copy(result.at[block], out_ref.at[block], done.at[block])
+
         for group in range(groups):
             tiles = []
             for block in range(blocks):
-                for kind, mask in enumerate((signed, own)):
+                rows = [
+                    jnp.concatenate(
+                        [
+                            jnp.broadcast_to(
+                                side[kind, group, pl.ds(block, 1), :], (pair, lanes)
+                            )
+                            for kind in range(2)
+                        ],
+                        axis=0,
+                    )
+                    for side in (high, low)
+                ]
+                for mask in masks:
                     tiles.append(
                         jnp.concatenate(
-                            [
-                                (jnp.broadcast_to(
-                                    side[kind, group, pl.ds(block, 1), :], (freqs, lanes)
-                                ) * mask).astype(jnp.bfloat16)
-                                for side in (high, low)
-                            ],
-                            axis=1,
+                            [(both * mask).astype(jnp.bfloat16) for both in rows], axis=1
                         )
                     )
             values = modes_ref[group]
@@ -205,18 +228,16 @@
                 jnp.concatenate([values, values], axis=0),
                 preferred_element_type=jnp.float32,
             )
-            rebuilt[:, group * 2 * freqs : (group + 1) * 2 * freqs, :] = product.astype(
+            rebuilt[:, :, group * freqs : (group + 1) * freqs, :] = product.astype(
                 jnp.bfloat16
-            ).reshape(blocks, 2 * freqs, columns)
-        result[0] = jnp.zeros((half, columns), jnp.float32)
-
-        def send(block):
-            return pltpu.make_async_copy(result.at[block], out_ref.at[block], done.at[block])
-
+            ).reshape(blocks, 2, freqs, columns)
         for block in range(blocks):
-            series = jnp.dot(table_ref[...], rebuilt[block], preferred_element_type=jnp.float32)
-            result[block] += series[:half]
-            result[block + 1] = series[half:]
+            even, odd = (
+                jnp.dot(table_ref[i], rebuilt[block, i], preferred_element_type=jnp.float32)
+                for i in range(2)
+            )
+            result[block] += (even + odd) * first
+            result[block + 1] = (even - odd) * second
             send(block).start()
         send(blocks).start()
         for block in range(blocks + 1):
@@ -225,23 +246,23 @@
     return pl.pallas_call(
         kernel,
         out_shape=jax.ShapeDtypeStruct((blocks + 1, half, columns), jnp.float32),
-        in_specs=[pl.BlockSpec(memory_space=pltpu.VMEM)] * 3,
+        in_specs=[pl.BlockSpec(memory_space=pltpu.VMEM)] * 4,
         out_specs=pl.BlockSpec(memory_space=pl.ANY),
         scratch_shapes=[
             pltpu.VMEM((2, groups, blocks, lanes), jnp.float32),
             pltpu.VMEM((2, groups, blocks, lanes), jnp.float32),
-            pltpu.VMEM((blocks, 2 * length, columns), jnp.bfloat16),
+            pltpu.VMEM((blocks, 2, length, columns), jnp.bfloat16),
             pltpu.VMEM((blocks + 1, half, columns), jnp.float32),
             pltpu.SemaphoreType.DMA((blocks + 1,)),
         ],
         compiler_params=pltpu.CompilerParams(vmem_limit_bytes=32 * MIB),
         cost_estimate=pl.CostEstimate(
-            flops=4 * length * length * blocks * columns,
+            flops=2 * length * length * blocks * columns,
             transcendentals=0,
             bytes_accessed=4 * (blocks + 1) * half * columns,
         ),
         name="synthesize",
-    )(coefficients, moved_modes, table)
+    )(coefficients, moved_modes, table, window)
 
 
 def body(spectra, eigvecs, weights):
@@ -256,7 +277,7 @@
     filtered = synthesize(
         gathered,
         moved.reshape(groups, -1, moved.shape[-1]),
-        transform_table(groups * freqs, groups),
+        *transform_tables(groups * freqs, groups),
     )
     return filtered.reshape(-1, filtered.shape[-1])
 

time: 49.2 us -> 48.4 us (0.984)
  Pallas kernels: 9.78 us -> 8.93 us
    pallas_call x1, Pallas kernels: 4.51 us -> 3.83 us  [synthesize(): pl.pallas_call(kernel, out_shape=jax.ShapeDtypeStruct((blocks + 1, half,...]
where the time goes in v4:
time: 48.4 us; the launch traced here: 48.1 us
  starting transfers between devices  26.4 us (55%)
  waiting for transfers between devices  12.4 us (26%)
  Pallas kernels  8.93 us (18%)
    all_to_all x1, waiting for transfers between devices, body(): lax.all_to_all(copies, 'freq', split_axis=0, concat_axis=0, tiled=True)  8.06 us
    ppermute x4, starting transfers between devices, around(): return lax.ppermute(value, 'space', pairs)  7.17 us
    all_to_all x1, starting transfers between devices, body(): lax.all_to_all(pieces, 'freq', split_axis=0, concat_axis=0, tiled=True)  7.04 us
    all_to_all x1, starting transfers between devices, body(): lax.all_to_all(copies, 'freq', split_axis=0, concat_axis=0, tiled=True)  6.72 us
    ppermute x2, starting transfers between devices, beside(): return lax.ppermute(value, 'space', [(i, i ^ 1) for i in range(count)])  5.46 us
    pallas_call x1, Pallas kernels, project(): pl.pallas_call(kernel, out_shape=[jax.ShapeDtypeStruct((blocks, 2 * half)...  4.4 us
    pallas_call x1, Pallas kernels, synthesize(): pl.pallas_call(kernel, out_shape=jax.ShapeDtypeStruct((blocks + 1, half,...  3.83 us
    ppermute x4, waiting for transfers between devices, around(): return lax.ppermute(value, 'space', pairs)  2.23 us
  transfers between devices with their start and end apart: 8, of which 7 were waited for; matrix products, arithmetic and copies ran while one was open for 1% of the time, Pallas kernels for 1%

profile of v4, /device:TPU:96, one launch (start us, length us, event | category | flops | bytes accessed | tf_op | source)
XLA Modules:
  0.0 48.1 jit_solution(8093125910425124200)
XLA Ops:
  0.0 0.0 copy-start
  0.0 0.0 copy-start.1
  0.0 4.4 %project.1 = (f32[24,128]{1,0:T(8,128)S(1)}, bf16[16,2,16,4,256]{4,3,2,1,0:T(4,128)(2,1)}) custom-call(bf16[768,4096]{1,0:T(8,128)(2,1)} %bitcast.3, bf16[2,16,4,4096]{3,2,1,0:T(4,128)(2,1)} %eigvecs_hbm.1, bf16[32,128]{1,0:T(8,128)(2,1)} %bitcast.4), custom_call_target="tpu_custom_call" | custom-call | flops 50331648 | bytes 7340032 | tf_op jit(solution)/shard_map/project/pallas_call | solution.py:89
  4.4 7.0 %all-to-all-start = ((bf16[16,2,16,4,256]{4,3,2,1,0:T(4,128)(2,1)}), bf16[16,2,16,4,256]{4,3,2,1,0:T(4,128)(2,1)S(1)}, u32[]{:S(2)}, u32[]{:S(2)}) async-start(bf16[16,2,16,4,256]{4,3,2,1,0:T(4,128)(2,1)} %get-tuple-element.10), calls=%async_computation | async-start | bytes 2097152 | tf_op jit(solution)/shard_map/all_to_all | solution.py:273
  11.5 0.1 collective-permute-start
  11.6 1.2 %collective-permute-done = f32[24,128]{1,0:T(8,128)S(1)} collective-permute-done((f32[24,128]{1,0:T(8,128)S(1)}, f32[24,128]{1,0:T(8,128)S(1)}, u32[]{:S(2)}, u32[]{:S(2)}) %collective-permute-start) | collective-permute-done | bytes 12320 | tf_op jit(solution)/shard_map/ppermute | solution.py:142
  12.7 4.5 %collective-permute-start.4 = (f32[24,128]{1,0:T(8,128)S(1)}, f32[24,128]{1,0:T(8,128)S(1)}, u32[]{:S(2)}, u32[]{:S(2)}) collective-permute-start(f32[24,128]{1,0:T(8,128)S(1)} %add.12.chip_ref), channel_id=1, source_target_pairs={{0,8},{2,10},{4,12},{6,14},{8,0},{10,2},{12,4},{14,6},{1,11},{3,13... | collective-permute-start | bytes 36872 | tf_op jit(solution)/shard_map/ppermute | solution.py:151
  17.2 0.0 collective-permute-start.3
  17.2 2.0 %collective-permute-start.2 = (f32[24,128]{1,0:T(8,128)S(1)}, f32[24,128]{1,0:T(8,128)S(1)}, u32[]{:S(2)}, u32[]{:S(2)}) collective-permute-start(f32[24,128]{1,0:T(8,128)S(1)} %add.12.chip_ref), channel_id=1, source_target_pairs={{0,14},{2,0},{4,2},{6,4},{8,6},{10,8},{12,10},{14,12},{1,5},{3,7},... | collective-permute-start | bytes 36872 | tf_op jit(solution)/shard_map/ppermute | solution.py:151
  19.3 0.7 %collective-permute-start.1 = (f32[24,128]{1,0:T(8,128)S(1)}, f32[24,128]{1,0:T(8,128)S(1)}, u32[]{:S(2)}, u32[]{:S(2)}) collective-permute-start(f32[24,128]{1,0:T(8,128)S(1)} %add.12.chip_ref), channel_id=1, source_target_pairs={{1,13},{3,15},{5,1},{7,3},{9,5},{11,7},{13,9},{15,11},{17,29},{19,... | collective-permute-start | bytes 36872 | tf_op jit(solution)/shard_map/ppermute | solution.py:151
  19.9 0.4 collective-permute-done.4
  20.3 0.8 %collective-permute-done.3 = f32[24,128]{1,0:T(8,128)S(1)} collective-permute-done((f32[24,128]{1,0:T(8,128)S(1)}, f32[24,128]{1,0:T(8,128)S(1)}, u32[]{:S(2)}, u32[]{:S(2)}) %collective-permute-start.3) | collective-permute-done | bytes 12320 | tf_op jit(solution)/shard_map/ppermute | solution.py:151
  21.1 1.0 %collective-permute-done.2 = f32[24,128]{1,0:T(8,128)S(1)} collective-permute-done((f32[24,128]{1,0:T(8,128)S(1)}, f32[24,128]{1,0:T(8,128)S(1)}, u32[]{:S(2)}, u32[]{:S(2)}) %collective-permute-start.2) | collective-permute-done | bytes 12320 | tf_op jit(solution)/shard_map/ppermute | solution.py:151
  22.1 0.0 collective-permute-done.1
  22.1 5.4 %collective-permute-start.5 = (f32[24,128]{1,0:T(8,128)S(1)}, f32[24,128]{1,0:T(8,128)S(1)}, u32[]{:S(2)}, u32[]{:S(2)}) collective-permute-start(f32[24,128]{1,0:T(8,128)S(1)} %add_add_fusion.arrived_ref), channel_id=1, source_target_pairs={{0,1},{1,0},{2,3},{3,2},{4,5},{5,4},{6,7},{7,6},{8,9},{9,8},{10,11... | collective-permute-start | bytes 36872 | tf_op jit(solution)/shard_map/ppermute | solution.py:142
  27.5 0.8 %collective-permute-done.5.beside_ref = f32[24,128]{1,0:T(8,128)S(1)} collective-permute-done((f32[24,128]{1,0:T(8,128)S(1)}, f32[24,128]{1,0:T(8,128)S(1)}, u32[]{:S(2)}, u32[]{:S(2)}) %collective-permute-start.5) | collective-permute-done | bytes 12320 | tf_op jit(solution)/shard_map/ppermute | solution.py:142
  28.4 0.7 %gather_terms.1 = f32[16,24,128]{2,1,0:T(8,128)} custom-call(f32[24,128]{1,0:T(8,128)S(1)} %add.12.chip_ref, f32[24,128]{1,0:T(8,128)S(1)} %add_add_fusion.arrived_ref, f32[24,128]{1,0:T(8,128)S(1)} %collective-permute-done.5.beside_ref), custom_call_target="tpu_custom_call" | custom-call | flops 9216 | bytes 196608 | tf_op jit(solution)/shard_map/gather_terms/pallas_call | solution.py:124
  29.0 0.1 all-to-all-done
  29.2 6.7 %all-to-all-start.1 = ((f32[16,24,128]{2,1,0:T(8,128)}), f32[16,24,128]{2,1,0:T(8,128)S(1)}, u32[]{:S(2)}, u32[]{:S(2)}) async-start(f32[16,24,128]{2,1,0:T(8,128)} %gather_terms.1), calls=%async_computation.1 | async-start | bytes 393216 | tf_op jit(solution)/shard_map/all_to_all | solution.py:276
  35.9 0.3 reshape.14.modes_ref
  36.2 8.1 %all-to-all-done.1.coef_ref = f32[16,24,128]{2,1,0:T(8,128)S(1)} async-done(((f32[16,24,128]{2,1,0:T(8,128)}), f32[16,24,128]{2,1,0:T(8,128)S(1)}, u32[]{:S(2)}, u32[]{:S(2)}) %all-to-all-start.1) | async-done | bytes 196640 | tf_op jit(solution)/shard_map/all_to_all | solution.py:276
  44.3 0.0 copy-done
  44.3 0.0 copy-done.1
  44.3 3.8 %synthesize.1 = f32[25,128,256]{2,1,0:T(8,128)} custom-call(f32[16,24,128]{2,1,0:T(8,128)S(1)} %all-to-all-done.1.coef_ref, bf16[16,128,256]{2,1,0:T(8,128)(2,1)S(1)} %reshape.14.modes_ref, bf16[2,128,256]{2,1,0:T(8,128)(2,1)S(1)} %copy-done.1, f32[2,128,128]{2,1,0:T(8,128)S(1)} %copy-done), custom_call_target="tpu_custom_call" | custom-call | flops 805306368 | bytes 3276800 | tf_op jit(solution)/shard_map/synthesize/pallas_call | solution.py:246
  (2 shorter events, 0.0 us)
Async XLA Ops:
  0.0 44.3 %copy-start = (f32[2,128,128]{2,1,0:T(8,128)S(1)}, f32[2,128,128]{2,1,0:T(8,128)}, u32[]{:S(2)}) copy-start(f32[2,128,128]{2,1,0:T(8,128)} %constant.5.clone.window_ref) | copy-start | bytes 393220
  0.0 44.3 %copy-start.1 = (bf16[2,128,256]{2,1,0:T(8,128)(2,1)S(1)}, bf16[2,128,256]{2,1,0:T(8,128)(2,1)}, u32[]{:S(2)}) copy-start(bf16[2,128,256]{2,1,0:T(8,128)(2,1)} %constant.4.clone.table_ref) | copy-start | bytes 393220
  4.4 24.8 %all-to-all-start = ((bf16[16,2,16,4,256]{4,3,2,1,0:T(4,128)(2,1)}), bf16[16,2,16,4,256]{4,3,2,1,0:T(4,128)(2,1)S(1)}, u32[]{:S(2)}, u32[]{:S(2)}) async-start(bf16[16,2,16,4,256]{4,3,2,1,0:T(4,128)(2,1)} %get-tuple-element.10), calls=%async_computation | async-start | bytes 2097152 | tf_op jit(solution)/shard_map/all_to_all | solution.py:273
  11.5 1.3 %collective-permute-start = (f32[24,128]{1,0:T(8,128)S(1)}, f32[24,128]{1,0:T(8,128)S(1)}, u32[]{:S(2)}, u32[]{:S(2)}) collective-permute-start(f32[24,128]{1,0:T(8,128)S(1)} %get-tuple-element.9), channel_id=1, source_target_pairs={{0,1},{1,0},{2,3},{3,2},{4,5},{5,4},{6,7},{7,6},{8,9},{9,8},{10,11... | collective-permute-start | bytes 36872 | tf_op jit(solution)/shard_map/ppermute | solution.py:142
  12.7 7.6 %collective-permute-start.4 = (f32[24,128]{1,0:T(8,128)S(1)}, f32[24,128]{1,0:T(8,128)S(1)}, u32[]{:S(2)}, u32[]{:S(2)}) collective-permute-start(f32[24,128]{1,0:T(8,128)S(1)} %add.12.chip_ref), channel_id=1, source_target_pairs={{0,8},{2,10},{4,12},{6,14},{8,0},{10,2},{12,4},{14,6},{1,11},{3,13... | collective-permute-start | bytes 36872 | tf_op jit(solution)/shard_map/ppermute | solution.py:151
  17.2 3.9 %collective-permute-start.3 = (f32[24,128]{1,0:T(8,128)S(1)}, f32[24,128]{1,0:T(8,128)S(1)}, u32[]{:S(2)}, u32[]{:S(2)}) collective-permute-start(f32[24,128]{1,0:T(8,128)S(1)} %add.12.chip_ref), channel_id=1, source_target_pairs={{0,2},{2,4},{4,6},{6,8},{8,10},{10,12},{12,14},{14,0},{1,7},{3,9},... | collective-permute-start | bytes 36872 | tf_op jit(solution)/shard_map/ppermute | solution.py:151
  17.2 4.9 %collective-permute-start.2 = (f32[24,128]{1,0:T(8,128)S(1)}, f32[24,128]{1,0:T(8,128)S(1)}, u32[]{:S(2)}, u32[]{:S(2)}) collective-permute-start(f32[24,128]{1,0:T(8,128)S(1)} %add.12.chip_ref), channel_id=1, source_target_pairs={{0,14},{2,0},{4,2},{6,4},{8,6},{10,8},{12,10},{14,12},{1,5},{3,7},... | collective-permute-start | bytes 36872 | tf_op jit(solution)/shard_map/ppermute | solution.py:151
  19.3 2.9 %collective-permute-start.1 = (f32[24,128]{1,0:T(8,128)S(1)}, f32[24,128]{1,0:T(8,128)S(1)}, u32[]{:S(2)}, u32[]{:S(2)}) collective-permute-start(f32[24,128]{1,0:T(8,128)S(1)} %add.12.chip_ref), channel_id=1, source_target_pairs={{1,13},{3,15},{5,1},{7,3},{9,5},{11,7},{13,9},{15,11},{17,29},{19,... | collective-permute-start | bytes 36872 | tf_op jit(solution)/shard_map/ppermute | solution.py:151
  22.1 6.2 %collective-permute-start.5 = (f32[24,128]{1,0:T(8,128)S(1)}, f32[24,128]{1,0:T(8,128)S(1)}, u32[]{:S(2)}, u32[]{:S(2)}) collective-permute-start(f32[24,128]{1,0:T(8,128)S(1)} %add_add_fusion.arrived_ref), channel_id=1, source_target_pairs={{0,1},{1,0},{2,3},{3,2},{4,5},{5,4},{6,7},{7,6},{8,9},{9,8},{10,11... | collective-permute-start | bytes 36872 | tf_op jit(solution)/shard_map/ppermute | solution.py:142
  29.2 15.1 %all-to-all-start.1 = ((f32[16,24,128]{2,1,0:T(8,128)}), f32[16,24,128]{2,1,0:T(8,128)S(1)}, u32[]{:S(2)}, u32[]{:S(2)}) async-start(f32[16,24,128]{2,1,0:T(8,128)} %gather_terms.1), calls=%async_computation.1 | async-start | bytes 393216 | tf_op jit(solution)/shard_map/all_to_all | solution.py:276

commit v5 on v4

--- a/solution.py
+++ b/solution.py
@@ -11,7 +11,7 @@
 MIB = 1024 * 1024
 LANES = 128
 SLAB = 4
-HOPS_BY_CORE = ((0, -2), (-1, 2), (1, 3), (4, -3))
+HOPS_BY_CORE = ((0, 1), (-1, 2), (-2, -3), (4, 3))
 
 
 def project(spectra, eigvecs, weights, parts):

time: 48.4 us -> 47.1 us (0.973)
  the two profiles are of different devices: /device:TPU:96 before, /device:TPU:1 now
where the time goes in v5:
time: 47.1 us; the launch traced here: 46.8 us
  starting transfers between devices  25.5 us (54%)
  waiting for transfers between devices  12 us (25%)
  Pallas kernels  8.93 us (19%)
    ppermute x4, starting transfers between devices, around(): return lax.ppermute(value, 'space', pairs)  10.3 us
    all_to_all x1, starting transfers between devices, body(): lax.all_to_all(pieces, 'freq', split_axis=0, concat_axis=0, tiled=True)  7.6 us
    all_to_all x1, waiting for transfers between devices, body(): lax.all_to_all(copies, 'freq', split_axis=0, concat_axis=0, tiled=True)  6.7 us
    all_to_all x1, starting transfers between devices, body(): lax.all_to_all(copies, 'freq', split_axis=0, concat_axis=0, tiled=True)  6.56 us
    pallas_call x1, Pallas kernels, project(): pl.pallas_call(kernel, out_shape=[jax.ShapeDtypeStruct((blocks, 2 * half)...  4.4 us
    pallas_call x1, Pallas kernels, synthesize(): pl.pallas_call(kernel, out_shape=jax.ShapeDtypeStruct((blocks + 1, half,...  3.84 us
    ppermute x4, waiting for transfers between devices, around(): return lax.ppermute(value, 'space', pairs)  3.28 us
    ppermute x2, waiting for transfers between devices, beside(): return lax.ppermute(value, 'space', [(i, i ^ 1) for i in range(count)])  2.01 us
  transfers between devices with their start and end apart: 8, of which 5 were waited for; matrix products, arithmetic and copies ran while one was open for 1% of the time, Pallas kernels for 1%

profile of v5, /device:TPU:1, one launch (start us, length us, event | category | flops | bytes accessed | tf_op | source)
XLA Modules:
  0.0 46.8 jit_solution(9366984977055252647)
XLA Ops:
  0.0 0.0 copy-start
  0.0 0.0 copy-start.1
  0.0 4.4 %project.1 = (f32[24,128]{1,0:T(8,128)S(1)}, bf16[16,2,16,4,256]{4,3,2,1,0:T(4,128)(2,1)}) custom-call(bf16[768,4096]{1,0:T(8,128)(2,1)} %bitcast.3, bf16[2,16,4,4096]{3,2,1,0:T(4,128)(2,1)} %eigvecs_hbm.1, bf16[32,128]{1,0:T(8,128)(2,1)} %bitcast.4), custom_call_target="tpu_custom_call" | custom-call | flops 50331648 | bytes 7340032 | tf_op jit(solution)/shard_map/project/pallas_call | solution.py:89
  4.4 7.6 %all-to-all-start = ((bf16[16,2,16,4,256]{4,3,2,1,0:T(4,128)(2,1)}), bf16[16,2,16,4,256]{4,3,2,1,0:T(4,128)(2,1)S(1)}, u32[]{:S(2)}, u32[]{:S(2)}) async-start(bf16[16,2,16,4,256]{4,3,2,1,0:T(4,128)(2,1)} %get-tuple-element.10), calls=%async_computation | async-start | bytes 2097152 | tf_op jit(solution)/shard_map/all_to_all | solution.py:273
  12.0 1.0 %collective-permute-start = (f32[24,128]{1,0:T(8,128)S(1)}, f32[24,128]{1,0:T(8,128)S(1)}, u32[]{:S(2)}, u32[]{:S(2)}) collective-permute-start(f32[24,128]{1,0:T(8,128)S(1)} %get-tuple-element.9), channel_id=1, source_target_pairs={{0,1},{1,0},{2,3},{3,2},{4,5},{5,4},{6,7},{7,6},{8,9},{9,8},{10,11... | collective-permute-start | bytes 36872 | tf_op jit(solution)/shard_map/ppermute | solution.py:142
  13.1 0.8 %collective-permute-done = f32[24,128]{1,0:T(8,128)S(1)} collective-permute-done((f32[24,128]{1,0:T(8,128)S(1)}, f32[24,128]{1,0:T(8,128)S(1)}, u32[]{:S(2)}, u32[]{:S(2)}) %collective-permute-start) | collective-permute-done | bytes 12320 | tf_op jit(solution)/shard_map/ppermute | solution.py:142
  13.9 4.3 %collective-permute-start.4 = (f32[24,128]{1,0:T(8,128)S(1)}, f32[24,128]{1,0:T(8,128)S(1)}, u32[]{:S(2)}, u32[]{:S(2)}) collective-permute-start(f32[24,128]{1,0:T(8,128)S(1)} %add.12.chip_ref), channel_id=1, source_target_pairs={{0,8},{2,10},{4,12},{6,14},{8,0},{10,2},{12,4},{14,6},{1,7},{3,9},... | collective-permute-start | bytes 36872 | tf_op jit(solution)/shard_map/ppermute | solution.py:151
  18.2 2.1 %collective-permute-start.3 = (f32[24,128]{1,0:T(8,128)S(1)}, f32[24,128]{1,0:T(8,128)S(1)}, u32[]{:S(2)}, u32[]{:S(2)}) collective-permute-start(f32[24,128]{1,0:T(8,128)S(1)} %add.12.chip_ref), channel_id=1, source_target_pairs={{0,12},{2,14},{4,0},{6,2},{8,4},{10,6},{12,8},{14,10},{1,11},{3,13... | collective-permute-start | bytes 36872 | tf_op jit(solution)/shard_map/ppermute | solution.py:151
  20.4 1.2 %collective-permute-start.2 = (f32[24,128]{1,0:T(8,128)S(1)}, f32[24,128]{1,0:T(8,128)S(1)}, u32[]{:S(2)}, u32[]{:S(2)}) collective-permute-start(f32[24,128]{1,0:T(8,128)S(1)} %add.12.chip_ref), channel_id=1, source_target_pairs={{0,14},{2,0},{4,2},{6,4},{8,6},{10,8},{12,10},{14,12},{1,5},{3,7},... | collective-permute-start | bytes 36872 | tf_op jit(solution)/shard_map/ppermute | solution.py:151
  21.6 2.6 %collective-permute-start.1 = (f32[24,128]{1,0:T(8,128)S(1)}, f32[24,128]{1,0:T(8,128)S(1)}, u32[]{:S(2)}, u32[]{:S(2)}) collective-permute-start(f32[24,128]{1,0:T(8,128)S(1)} %add.12.chip_ref), channel_id=1, source_target_pairs={{1,3},{3,5},{5,7},{7,9},{9,11},{11,13},{13,15},{15,1},{17,19},{19,... | collective-permute-start | bytes 36872 | tf_op jit(solution)/shard_map/ppermute | solution.py:151
  24.2 0.0 collective-permute-done.4
  24.2 0.0 collective-permute-done.3
  24.2 1.6 %collective-permute-done.2 = f32[24,128]{1,0:T(8,128)S(1)} collective-permute-done((f32[24,128]{1,0:T(8,128)S(1)}, f32[24,128]{1,0:T(8,128)S(1)}, u32[]{:S(2)}, u32[]{:S(2)}) %collective-permute-start.2) | collective-permute-done | bytes 12320 | tf_op jit(solution)/shard_map/ppermute | solution.py:151
  25.8 1.7 %collective-permute-done.1 = f32[24,128]{1,0:T(8,128)S(1)} collective-permute-done((f32[24,128]{1,0:T(8,128)S(1)}, f32[24,128]{1,0:T(8,128)S(1)}, u32[]{:S(2)}, u32[]{:S(2)}) %collective-permute-start.1) | collective-permute-done | bytes 12320 | tf_op jit(solution)/shard_map/ppermute | solution.py:151
  27.5 0.0 collective-permute-start.5
  27.5 1.2 %collective-permute-done.5.beside_ref = f32[24,128]{1,0:T(8,128)S(1)} collective-permute-done((f32[24,128]{1,0:T(8,128)S(1)}, f32[24,128]{1,0:T(8,128)S(1)}, u32[]{:S(2)}, u32[]{:S(2)}) %collective-permute-start.5) | collective-permute-done | bytes 12320 | tf_op jit(solution)/shard_map/ppermute | solution.py:142
  28.7 0.7 %gather_terms.1 = f32[16,24,128]{2,1,0:T(8,128)} custom-call(f32[24,128]{1,0:T(8,128)S(1)} %add.12.chip_ref, f32[24,128]{1,0:T(8,128)S(1)} %add_add_fusion.arrived_ref, f32[24,128]{1,0:T(8,128)S(1)} %collective-permute-done.5.beside_ref), custom_call_target="tpu_custom_call" | custom-call | flops 9216 | bytes 196608 | tf_op jit(solution)/shard_map/gather_terms/pallas_call | solution.py:124
  29.4 0.0 all-to-all-done
  29.4 6.6 %all-to-all-start.1 = ((f32[16,24,128]{2,1,0:T(8,128)}), f32[16,24,128]{2,1,0:T(8,128)S(1)}, u32[]{:S(2)}, u32[]{:S(2)}) async-start(f32[16,24,128]{2,1,0:T(8,128)} %gather_terms.1), calls=%async_computation.1 | async-start | bytes 393216 | tf_op jit(solution)/shard_map/all_to_all | solution.py:276
  35.9 0.3 reshape.14.modes_ref
  36.2 6.7 %all-to-all-done.1.coef_ref = f32[16,24,128]{2,1,0:T(8,128)S(1)} async-done(((f32[16,24,128]{2,1,0:T(8,128)}), f32[16,24,128]{2,1,0:T(8,128)S(1)}, u32[]{:S(2)}, u32[]{:S(2)}) %all-to-all-start.1) | async-done | bytes 196640 | tf_op jit(solution)/shard_map/all_to_all | solution.py:276
  42.9 0.0 copy-done
  42.9 0.0 copy-done.1
  42.9 3.8 %synthesize.1 = f32[25,128,256]{2,1,0:T(8,128)} custom-call(f32[16,24,128]{2,1,0:T(8,128)S(1)} %all-to-all-done.1.coef_ref, bf16[16,128,256]{2,1,0:T(8,128)(2,1)S(1)} %reshape.14.modes_ref, bf16[2,128,256]{2,1,0:T(8,128)(2,1)S(1)} %copy-done.1, f32[2,128,128]{2,1,0:T(8,128)S(1)} %copy-done), custom_call_target="tpu_custom_call" | custom-call | flops 805306368 | bytes 3276800 | tf_op jit(solution)/shard_map/synthesize/pallas_call | solution.py:246
  (2 shorter events, 0.0 us)
Async XLA Ops:
  0.0 42.9 %copy-start = (f32[2,128,128]{2,1,0:T(8,128)S(1)}, f32[2,128,128]{2,1,0:T(8,128)}, u32[]{:S(2)}) copy-start(f32[2,128,128]{2,1,0:T(8,128)} %constant.5.clone.window_ref) | copy-start | bytes 393220
  0.0 42.9 %copy-start.1 = (bf16[2,128,256]{2,1,0:T(8,128)(2,1)S(1)}, bf16[2,128,256]{2,1,0:T(8,128)(2,1)}, u32[]{:S(2)}) copy-start(bf16[2,128,256]{2,1,0:T(8,128)(2,1)} %constant.4.clone.table_ref) | copy-start | bytes 393220
  4.4 25.0 %all-to-all-start = ((bf16[16,2,16,4,256]{4,3,2,1,0:T(4,128)(2,1)}), bf16[16,2,16,4,256]{4,3,2,1,0:T(4,128)(2,1)S(1)}, u32[]{:S(2)}, u32[]{:S(2)}) async-start(bf16[16,2,16,4,256]{4,3,2,1,0:T(4,128)(2,1)} %get-tuple-element.10), calls=%async_computation | async-start | bytes 2097152 | tf_op jit(solution)/shard_map/all_to_all | solution.py:273
  12.0 1.9 %collective-permute-start = (f32[24,128]{1,0:T(8,128)S(1)}, f32[24,128]{1,0:T(8,128)S(1)}, u32[]{:S(2)}, u32[]{:S(2)}) collective-permute-start(f32[24,128]{1,0:T(8,128)S(1)} %get-tuple-element.9), channel_id=1, source_target_pairs={{0,1},{1,0},{2,3},{3,2},{4,5},{5,4},{6,7},{7,6},{8,9},{9,8},{10,11... | collective-permute-start | bytes 36872 | tf_op jit(solution)/shard_map/ppermute | solution.py:142
  13.9 10.3 %collective-permute-start.4 = (f32[24,128]{1,0:T(8,128)S(1)}, f32[24,128]{1,0:T(8,128)S(1)}, u32[]{:S(2)}, u32[]{:S(2)}) collective-permute-start(f32[24,128]{1,0:T(8,128)S(1)} %add.12.chip_ref), channel_id=1, source_target_pairs={{0,8},{2,10},{4,12},{6,14},{8,0},{10,2},{12,4},{14,6},{1,7},{3,9},... | collective-permute-start | bytes 36872 | tf_op jit(solution)/shard_map/ppermute | solution.py:151
  18.2 6.0 %collective-permute-start.3 = (f32[24,128]{1,0:T(8,128)S(1)}, f32[24,128]{1,0:T(8,128)S(1)}, u32[]{:S(2)}, u32[]{:S(2)}) collective-permute-start(f32[24,128]{1,0:T(8,128)S(1)} %add.12.chip_ref), channel_id=1, source_target_pairs={{0,12},{2,14},{4,0},{6,2},{8,4},{10,6},{12,8},{14,10},{1,11},{3,13... | collective-permute-start | bytes 36872 | tf_op jit(solution)/shard_map/ppermute | solution.py:151
  20.4 5.4 %collective-permute-start.2 = (f32[24,128]{1,0:T(8,128)S(1)}, f32[24,128]{1,0:T(8,128)S(1)}, u32[]{:S(2)}, u32[]{:S(2)}) collective-permute-start(f32[24,128]{1,0:T(8,128)S(1)} %add.12.chip_ref), channel_id=1, source_target_pairs={{0,14},{2,0},{4,2},{6,4},{8,6},{10,8},{12,10},{14,12},{1,5},{3,7},... | collective-permute-start | bytes 36872 | tf_op jit(solution)/shard_map/ppermute | solution.py:151
  21.6 5.9 %collective-permute-start.1 = (f32[24,128]{1,0:T(8,128)S(1)}, f32[24,128]{1,0:T(8,128)S(1)}, u32[]{:S(2)}, u32[]{:S(2)}) collective-permute-start(f32[24,128]{1,0:T(8,128)S(1)} %add.12.chip_ref), channel_id=1, source_target_pairs={{1,3},{3,5},{5,7},{7,9},{9,11},{11,13},{13,15},{15,1},{17,19},{19,... | collective-permute-start | bytes 36872 | tf_op jit(solution)/shard_map/ppermute | solution.py:151
  27.5 1.2 %collective-permute-start.5 = (f32[24,128]{1,0:T(8,128)S(1)}, f32[24,128]{1,0:T(8,128)S(1)}, u32[]{:S(2)}, u32[]{:S(2)}) collective-permute-start(f32[24,128]{1,0:T(8,128)S(1)} %add_add_fusion.arrived_ref), channel_id=1, source_target_pairs={{0,1},{1,0},{2,3},{3,2},{4,5},{5,4},{6,7},{7,6},{8,9},{9,8},{10,11... | collective-permute-start | bytes 36872 | tf_op jit(solution)/shard_map/ppermute | solution.py:142
  29.4 13.6 %all-to-all-start.1 = ((f32[16,24,128]{2,1,0:T(8,128)}), f32[16,24,128]{2,1,0:T(8,128)S(1)}, u32[]{:S(2)}, u32[]{:S(2)}) async-start(f32[16,24,128]{2,1,0:T(8,128)} %gather_terms.1), calls=%async_computation.1 | async-start | bytes 393216 | tf_op jit(solution)/shard_map/all_to_all | solution.py:276

commit v6 on v5

--- a/solution.py
+++ b/solution.py
@@ -53,23 +53,24 @@
                 weighted[first : first + modes] = (
                     eigvecs_ref[part, k].astype(jnp.float32) * scale
                 )
-        columns[...] = jnp.transpose(weighted[...]).astype(dtype)
+        columns[...] = jnp.transpose(weighted[...].astype(dtype))
         slabs = []
-        for piece in range(parts):
-            pieces_ref[piece] = eigvecs_ref[:, :, :, piece * width : (piece + 1) * width]
-            if piece % SLAB == SLAB - 1:
-                some = pl.ds(piece + 1 - SLAB, SLAB)
-                slabs.append(
-                    pltpu.make_async_copy(
-                        pieces_ref.at[some], pieces_hbm.at[some], sent.at[len(slabs)]
-                    )
-                )
-                slabs[-1].start()
         for copy, start, end in zip(by_rows, starts, ends):
             copy.wait()
             total[start:end] = jnp.dot(
                 spectra_ref[start:end], columns[...], preferred_element_type=jnp.float32
             )
+            if start == 0:
+                for piece in range(parts):
+                    pieces_ref[piece] = eigvecs_ref[:, :, :, piece * width : (piece + 1) * width]
+                    if piece % SLAB == SLAB - 1:
+                        some = pl.ds(piece + 1 - SLAB, SLAB)
+                        slabs.append(
+                            pltpu.make_async_copy(
+                                pieces_ref.at[some], pieces_hbm.at[some], sent.at[len(slabs)]
+                            )
+                        )
+                        slabs[-1].start()
         lane = lax.broadcasted_iota(jnp.int32, (blocks, 2 * half), 1)
         sums = []
         for part in range(2):

time: 47.1 us -> 47.1 us (level)
  no operation moved by 1% of the time
where the time goes in v6:
time: 47.1 us; the launch traced here: 46.7 us
  starting transfers between devices  25.5 us (54%)
  waiting for transfers between devices  12 us (25%)
  Pallas kernels  8.85 us (19%)
    ppermute x4, starting transfers between devices, around(): return lax.ppermute(value, 'space', pairs)  10.3 us
    all_to_all x1, starting transfers between devices, body(): lax.all_to_all(pieces, 'freq', split_axis=0, concat_axis=0, tiled=True)  7.6 us
    all_to_all x1, waiting for transfers between devices, body(): lax.all_to_all(copies, 'freq', split_axis=0, concat_axis=0, tiled=True)  6.7 us
    all_to_all x1, starting transfers between devices, body(): lax.all_to_all(copies, 'freq', split_axis=0, concat_axis=0, tiled=True)  6.56 us
    pallas_call x1, Pallas kernels, project(): pl.pallas_call(kernel, out_shape=[jax.ShapeDtypeStruct((blocks, 2 * half)...  4.32 us
    pallas_call x1, Pallas kernels, synthesize(): pl.pallas_call(kernel, out_shape=jax.ShapeDtypeStruct((blocks + 1, half,...  3.83 us
    ppermute x4, waiting for transfers between devices, around(): return lax.ppermute(value, 'space', pairs)  3.28 us
    ppermute x2, waiting for transfers between devices, beside(): return lax.ppermute(value, 'space', [(i, i ^ 1) for i in range(count)])  2.01 us
  transfers between devices with their start and end apart: 8, of which 5 were waited for; matrix products, arithmetic and copies ran while one was open for 1% of the time, Pallas kernels for 1%

profile of v6, /device:TPU:1, one launch (start us, length us, event | category | flops | bytes accessed | tf_op | source)
XLA Modules:
  0.0 46.7 jit_solution(8413020583064761607)
XLA Ops:
  0.0 0.0 copy-start
  0.0 0.0 copy-start.1
  0.0 4.3 %project.1 = (f32[24,128]{1,0:T(8,128)S(1)}, bf16[16,2,16,4,256]{4,3,2,1,0:T(4,128)(2,1)}) custom-call(bf16[768,4096]{1,0:T(8,128)(2,1)} %bitcast.3, bf16[2,16,4,4096]{3,2,1,0:T(4,128)(2,1)} %eigvecs_hbm.1, bf16[32,128]{1,0:T(8,128)(2,1)} %bitcast.4), custom_call_target="tpu_custom_call" | custom-call | flops 50331648 | bytes 7340032 | tf_op jit(solution)/shard_map/project/pallas_call | solution.py:90
  4.3 7.6 %all-to-all-start = ((bf16[16,2,16,4,256]{4,3,2,1,0:T(4,128)(2,1)}), bf16[16,2,16,4,256]{4,3,2,1,0:T(4,128)(2,1)S(1)}, u32[]{:S(2)}, u32[]{:S(2)}) async-start(bf16[16,2,16,4,256]{4,3,2,1,0:T(4,128)(2,1)} %get-tuple-element.10), calls=%async_computation | async-start | bytes 2097152 | tf_op jit(solution)/shard_map/all_to_all | solution.py:274
  11.9 1.0 %collective-permute-start = (f32[24,128]{1,0:T(8,128)S(1)}, f32[24,128]{1,0:T(8,128)S(1)}, u32[]{:S(2)}, u32[]{:S(2)}) collective-permute-start(f32[24,128]{1,0:T(8,128)S(1)} %get-tuple-element.9), channel_id=1, source_target_pairs={{0,1},{1,0},{2,3},{3,2},{4,5},{5,4},{6,7},{7,6},{8,9},{9,8},{10,11... | collective-permute-start | bytes 36872 | tf_op jit(solution)/shard_map/ppermute | solution.py:143
  13.0 0.8 %collective-permute-done = f32[24,128]{1,0:T(8,128)S(1)} collective-permute-done((f32[24,128]{1,0:T(8,128)S(1)}, f32[24,128]{1,0:T(8,128)S(1)}, u32[]{:S(2)}, u32[]{:S(2)}) %collective-permute-start) | collective-permute-done | bytes 12320 | tf_op jit(solution)/shard_map/ppermute | solution.py:143
  13.8 4.3 %collective-permute-start.4 = (f32[24,128]{1,0:T(8,128)S(1)}, f32[24,128]{1,0:T(8,128)S(1)}, u32[]{:S(2)}, u32[]{:S(2)}) collective-permute-start(f32[24,128]{1,0:T(8,128)S(1)} %add.12.chip_ref), channel_id=1, source_target_pairs={{0,8},{2,10},{4,12},{6,14},{8,0},{10,2},{12,4},{14,6},{1,7},{3,9},... | collective-permute-start | bytes 36872 | tf_op jit(solution)/shard_map/ppermute | solution.py:152
  18.2 2.1 %collective-permute-start.3 = (f32[24,128]{1,0:T(8,128)S(1)}, f32[24,128]{1,0:T(8,128)S(1)}, u32[]{:S(2)}, u32[]{:S(2)}) collective-permute-start(f32[24,128]{1,0:T(8,128)S(1)} %add.12.chip_ref), channel_id=1, source_target_pairs={{0,12},{2,14},{4,0},{6,2},{8,4},{10,6},{12,8},{14,10},{1,11},{3,13... | collective-permute-start | bytes 36872 | tf_op jit(solution)/shard_map/ppermute | solution.py:152
  20.3 1.2 %collective-permute-start.2 = (f32[24,128]{1,0:T(8,128)S(1)}, f32[24,128]{1,0:T(8,128)S(1)}, u32[]{:S(2)}, u32[]{:S(2)}) collective-permute-start(f32[24,128]{1,0:T(8,128)S(1)} %add.12.chip_ref), channel_id=1, source_target_pairs={{0,14},{2,0},{4,2},{6,4},{8,6},{10,8},{12,10},{14,12},{1,5},{3,7},... | collective-permute-start | bytes 36872 | tf_op jit(solution)/shard_map/ppermute | solution.py:152
  21.5 2.6 %collective-permute-start.1 = (f32[24,128]{1,0:T(8,128)S(1)}, f32[24,128]{1,0:T(8,128)S(1)}, u32[]{:S(2)}, u32[]{:S(2)}) collective-permute-start(f32[24,128]{1,0:T(8,128)S(1)} %add.12.chip_ref), channel_id=1, source_target_pairs={{1,3},{3,5},{5,7},{7,9},{9,11},{11,13},{13,15},{15,1},{17,19},{19,... | collective-permute-start | bytes 36872 | tf_op jit(solution)/shard_map/ppermute | solution.py:152
  24.1 0.0 collective-permute-done.4
  24.1 0.0 collective-permute-done.3
  24.1 1.6 %collective-permute-done.2 = f32[24,128]{1,0:T(8,128)S(1)} collective-permute-done((f32[24,128]{1,0:T(8,128)S(1)}, f32[24,128]{1,0:T(8,128)S(1)}, u32[]{:S(2)}, u32[]{:S(2)}) %collective-permute-start.2) | collective-permute-done | bytes 12320 | tf_op jit(solution)/shard_map/ppermute | solution.py:152
  25.7 1.7 %collective-permute-done.1 = f32[24,128]{1,0:T(8,128)S(1)} collective-permute-done((f32[24,128]{1,0:T(8,128)S(1)}, f32[24,128]{1,0:T(8,128)S(1)}, u32[]{:S(2)}, u32[]{:S(2)}) %collective-permute-start.1) | collective-permute-done | bytes 12320 | tf_op jit(solution)/shard_map/ppermute | solution.py:152
  27.4 0.0 collective-permute-start.5
  27.4 1.2 %collective-permute-done.5.beside_ref = f32[24,128]{1,0:T(8,128)S(1)} collective-permute-done((f32[24,128]{1,0:T(8,128)S(1)}, f32[24,128]{1,0:T(8,128)S(1)}, u32[]{:S(2)}, u32[]{:S(2)}) %collective-permute-start.5) | collective-permute-done | bytes 12320 | tf_op jit(solution)/shard_map/ppermute | solution.py:143
  28.6 0.7 %gather_terms.1 = f32[16,24,128]{2,1,0:T(8,128)} custom-call(f32[24,128]{1,0:T(8,128)S(1)} %add.12.chip_ref, f32[24,128]{1,0:T(8,128)S(1)} %add_add_fusion.arrived_ref, f32[24,128]{1,0:T(8,128)S(1)} %collective-permute-done.5.beside_ref), custom_call_target="tpu_custom_call" | custom-call | flops 9216 | bytes 196608 | tf_op jit(solution)/shard_map/gather_terms/pallas_call | solution.py:125
  29.3 0.0 all-to-all-done
  29.3 6.6 %all-to-all-start.1 = ((f32[16,24,128]{2,1,0:T(8,128)}), f32[16,24,128]{2,1,0:T(8,128)S(1)}, u32[]{:S(2)}, u32[]{:S(2)}) async-start(f32[16,24,128]{2,1,0:T(8,128)} %gather_terms.1), calls=%async_computation.1 | async-start | bytes 393216 | tf_op jit(solution)/shard_map/all_to_all | solution.py:277
  35.9 0.3 reshape.14.modes_ref
  36.2 6.7 %all-to-all-done.1.coef_ref = f32[16,24,128]{2,1,0:T(8,128)S(1)} async-done(((f32[16,24,128]{2,1,0:T(8,128)}), f32[16,24,128]{2,1,0:T(8,128)S(1)}, u32[]{:S(2)}, u32[]{:S(2)}) %all-to-all-start.1) | async-done | bytes 196640 | tf_op jit(solution)/shard_map/all_to_all | solution.py:277
  42.9 0.0 copy-done
  42.9 0.0 copy-done.1
  42.9 3.8 %synthesize.1 = f32[25,128,256]{2,1,0:T(8,128)} custom-call(f32[16,24,128]{2,1,0:T(8,128)S(1)} %all-to-all-done.1.coef_ref, bf16[16,128,256]{2,1,0:T(8,128)(2,1)S(1)} %reshape.14.modes_ref, bf16[2,128,256]{2,1,0:T(8,128)(2,1)S(1)} %copy-done.1, f32[2,128,128]{2,1,0:T(8,128)S(1)} %copy-done), custom_call_target="tpu_custom_call" | custom-call | flops 805306368 | bytes 3276800 | tf_op jit(solution)/shard_map/synthesize/pallas_call | solution.py:247
  (2 shorter events, 0.0 us)
Async XLA Ops:
  0.0 42.9 %copy-start = (f32[2,128,128]{2,1,0:T(8,128)S(1)}, f32[2,128,128]{2,1,0:T(8,128)}, u32[]{:S(2)}) copy-start(f32[2,128,128]{2,1,0:T(8,128)} %constant.5.clone.window_ref) | copy-start | bytes 393220
  0.0 42.9 %copy-start.1 = (bf16[2,128,256]{2,1,0:T(8,128)(2,1)S(1)}, bf16[2,128,256]{2,1,0:T(8,128)(2,1)}, u32[]{:S(2)}) copy-start(bf16[2,128,256]{2,1,0:T(8,128)(2,1)} %constant.4.clone.table_ref) | copy-start | bytes 393220
  4.3 25.0 %all-to-all-start = ((bf16[16,2,16,4,256]{4,3,2,1,0:T(4,128)(2,1)}), bf16[16,2,16,4,256]{4,3,2,1,0:T(4,128)(2,1)S(1)}, u32[]{:S(2)}, u32[]{:S(2)}) async-start(bf16[16,2,16,4,256]{4,3,2,1,0:T(4,128)(2,1)} %get-tuple-element.10), calls=%async_computation | async-start | bytes 2097152 | tf_op jit(solution)/shard_map/all_to_all | solution.py:274
  11.9 1.9 %collective-permute-start = (f32[24,128]{1,0:T(8,128)S(1)}, f32[24,128]{1,0:T(8,128)S(1)}, u32[]{:S(2)}, u32[]{:S(2)}) collective-permute-start(f32[24,128]{1,0:T(8,128)S(1)} %get-tuple-element.9), channel_id=1, source_target_pairs={{0,1},{1,0},{2,3},{3,2},{4,5},{5,4},{6,7},{7,6},{8,9},{9,8},{10,11... | collective-permute-start | bytes 36872 | tf_op jit(solution)/shard_map/ppermute | solution.py:143
  13.8 10.3 %collective-permute-start.4 = (f32[24,128]{1,0:T(8,128)S(1)}, f32[24,128]{1,0:T(8,128)S(1)}, u32[]{:S(2)}, u32[]{:S(2)}) collective-permute-start(f32[24,128]{1,0:T(8,128)S(1)} %add.12.chip_ref), channel_id=1, source_target_pairs={{0,8},{2,10},{4,12},{6,14},{8,0},{10,2},{12,4},{14,6},{1,7},{3,9},... | collective-permute-start | bytes 36872 | tf_op jit(solution)/shard_map/ppermute | solution.py:152
  18.2 6.0 %collective-permute-start.3 = (f32[24,128]{1,0:T(8,128)S(1)}, f32[24,128]{1,0:T(8,128)S(1)}, u32[]{:S(2)}, u32[]{:S(2)}) collective-permute-start(f32[24,128]{1,0:T(8,128)S(1)} %add.12.chip_ref), channel_id=1, source_target_pairs={{0,12},{2,14},{4,0},{6,2},{8,4},{10,6},{12,8},{14,10},{1,11},{3,13... | collective-permute-start | bytes 36872 | tf_op jit(solution)/shard_map/ppermute | solution.py:152
  20.3 5.4 %collective-permute-start.2 = (f32[24,128]{1,0:T(8,128)S(1)}, f32[24,128]{1,0:T(8,128)S(1)}, u32[]{:S(2)}, u32[]{:S(2)}) collective-permute-start(f32[24,128]{1,0:T(8,128)S(1)} %add.12.chip_ref), channel_id=1, source_target_pairs={{0,14},{2,0},{4,2},{6,4},{8,6},{10,8},{12,10},{14,12},{1,5},{3,7},... | collective-permute-start | bytes 36872 | tf_op jit(solution)/shard_map/ppermute | solution.py:152
  21.5 5.9 %collective-permute-start.1 = (f32[24,128]{1,0:T(8,128)S(1)}, f32[24,128]{1,0:T(8,128)S(1)}, u32[]{:S(2)}, u32[]{:S(2)}) collective-permute-start(f32[24,128]{1,0:T(8,128)S(1)} %add.12.chip_ref), channel_id=1, source_target_pairs={{1,3},{3,5},{5,7},{7,9},{9,11},{11,13},{13,15},{15,1},{17,19},{19,... | collective-permute-start | bytes 36872 | tf_op jit(solution)/shard_map/ppermute | solution.py:152
  27.4 1.2 %collective-permute-start.5 = (f32[24,128]{1,0:T(8,128)S(1)}, f32[24,128]{1,0:T(8,128)S(1)}, u32[]{:S(2)}, u32[]{:S(2)}) collective-permute-start(f32[24,128]{1,0:T(8,128)S(1)} %add_add_fusion.arrived_ref), channel_id=1, source_target_pairs={{0,1},{1,0},{2,3},{3,2},{4,5},{5,4},{6,7},{7,6},{8,9},{9,8},{10,11... | collective-permute-start | bytes 36872 | tf_op jit(solution)/shard_map/ppermute | solution.py:143
  29.3 13.6 %all-to-all-start.1 = ((f32[16,24,128]{2,1,0:T(8,128)}), f32[16,24,128]{2,1,0:T(8,128)S(1)}, u32[]{:S(2)}, u32[]{:S(2)}) async-start(f32[16,24,128]{2,1,0:T(8,128)} %gather_terms.1), calls=%async_computation.1 | async-start | bytes 393216 | tf_op jit(solution)/shard_map/all_to_all | solution.py:277
